TPU v7x, 512 devices: a whole 4x8x8 slice. The times are simulated.
512 devices in a mesh: rows: 64 (over y_hi, z, core), cols: 8 (over y_lo, x).
Axes of the slice: x: 4, y: 8 (y_hi: 4, y_lo: 2; y = y_hi * 2 + y_lo), z: 8, core: 2. Of those that a mesh axis runs over, the one named last changes fastest.
Arguments:
- residual: bfloat16 [2, 8192, 8192], P(None, 'rows', 'cols'), may hold values from -6 to 6
- field_slopes: bfloat16 [4, 8192, 8192], P(None, 'rows', 'cols'), may hold values from -6 to 6
- source_tile: int32 [2, 8192, 64], P(None, 'rows', 'cols'), may hold values from 0 to 7
- row_shift: int32 [2, 8192, 64], P(None, 'rows', 'cols'), may hold values from -8 to 8
- pixel_shift: int32 [2, 8192, 64], P(None, 'rows', 'cols'), may hold values from -2 to 2
- fraction: float32 [2, 8192, 64], P(None, 'rows', 'cols'), may hold values from 0 to 1
Outputs:
- potential_step: float32 [8192, 8192], P('rows', 'cols')
Inputs may be any that keep to these rules, and one draw needn't show every extreme that they name: `source_tile`: a tile number inside the group of 8 tiles that holds the destination tile.
All inputs are finite; a program needn't handle non-finite values.
Results may differ from a plain program's by a relative error of at most 0.0003.
Values may be sent and summed in bfloat16 or wider, within the bound.
A program may use at most 64 MiB of HBM per device.

v0:
```python
import math

import jax
import jax.numpy as jnp
from jax import lax
from jax.sharding import PartitionSpec as P

N = 8192
TILE = 128
PAIRS = 2
HALO = 8
SHIFT = 2


local_weight = 0.5
highest = lax.Precision.HIGHEST


def with_halo(x, sides, width):
    for axis, dim in sides:
        peers, length = (lax.axis_size(axis), x.shape[dim])
        up = [(i, (i + 1) % peers) for i in range(peers - 1)]
        down = [(j, i) for i, j in up]
        last = lax.slice_in_dim(x, length - width, length, axis=dim)
        first = lax.slice_in_dim(x, 0, width, axis=dim)
        before = lax.ppermute(last, axis, up)
        after = lax.ppermute(first, axis, down)
        x = jnp.concatenate([before, x, after], axis=dim)
    return x


def phase_pair(phases, length, direction):
    angles = phases.astype(jnp.float32) * (direction * 2.0 * math.pi / length)
    return (jnp.cos(angles), jnp.sin(angles))


def fourier_matrix(length, direction):
    counter = jnp.arange(length, dtype=jnp.int32)
    cosine, sine_part = phase_pair(counter[:, None] * counter[None, :] % length, length, direction)
    return jnp.stack([jnp.stack([cosine, sine_part], 1), jnp.stack([-sine_part, cosine], 1)], 0)


def rotate(values, cosine, sine_part):
    real_part = values[0] * cosine - values[1] * sine_part
    imag_part = values[0] * sine_part + values[1] * cosine
    return jnp.stack([real_part, imag_part])


def contract_indices(formula, values, matrix):
    return jnp.einsum(
        formula, values, matrix, precision=highest, preferred_element_type=jnp.float32
    )


def signed_wave(counter):
    middle = N // 2
    shifted = jnp.where(counter > middle, counter - N, counter)
    shifted = jnp.where(counter == middle, 0, shifted)
    return shifted.astype(jnp.float32) * (2.0 * math.pi / N)


def across_columns(values):
    return lax.all_to_all(values, "cols", split_axis=1, concat_axis=2, tiled=True)


def across_rows(values):
    return lax.all_to_all(values, "rows", split_axis=3, concat_axis=1, tiled=True)


def remap_tiles(padded, source_tile, row_shift, pixel_shift, fraction):
    rows_dev = padded.shape[1] - 2 * HALO
    tiles_dev = padded.shape[2] // TILE
    tile_rows = padded.reshape(2, (rows_dev + 2 * HALO) * tiles_dev, TILE)
    row_index = jnp.arange(rows_dev, dtype=jnp.int32)[None, :, None]
    flat_index = (row_index + HALO + row_shift) * tiles_dev + source_tile
    picked = jnp.take(tile_rows, flat_index.reshape(-1), axis=1)
    picked = picked.reshape(2, PAIRS, rows_dev, tiles_dev, TILE)
    widened = jnp.pad(picked, ((0, 0), (0, 0), (0, 0), (0, 0), (SHIFT + 1, SHIFT + 1)))
    pulled = jnp.zeros((2, rows_dev, tiles_dev, TILE), jnp.float32)
    for offset in range(-SHIFT, SHIFT + 2):
        weights = jnp.where(pixel_shift == offset, 1.0 - fraction, 0.0)
        weights = weights + jnp.where(pixel_shift + 1 == offset, fraction, 0.0)
        start_at = SHIFT + 1 + offset
        window = widened[..., start_at : start_at + TILE].astype(jnp.float32)
        pulled = pulled + jnp.sum(window * weights[None, :, :, :, None], axis=1)
    return pulled.reshape(2, rows_dev, tiles_dev * TILE)


def weigh_spectra(power_spectra, row_wave, col_wave):
    floored_wavenumber = 8.0 * math.pi / N
    weight = local_weight + 1.0 / (
        row_wave * row_wave + col_wave * col_wave + floored_wavenumber * floored_wavenumber
    )
    real_part = weight * (col_wave * power_spectra[1, 0] - row_wave * power_spectra[0, 0])
    imag_part = -weight * (col_wave * power_spectra[0, 0] + row_wave * power_spectra[1, 0])
    return jnp.stack([real_part, imag_part])


def per_device(residual, field_slopes, source_tile, row_shift, pixel_shift, fraction):
    padded = with_halo(residual, (("rows", 1),), HALO)
    pulled = remap_tiles(padded, source_tile, row_shift, pixel_shift, fraction)
    slopes = field_slopes.astype(jnp.float32)
    flow_across = -(pulled[0] * slopes[0] + pulled[1] * slopes[1])
    downward_flow = -(pulled[0] * slopes[2] + pulled[1] * slopes[3])
    rows_dev = residual.shape[1]
    cols_dev = residual.shape[2]
    rows_count = lax.axis_size("rows")
    cols_count = lax.axis_size("cols")
    part_rows = rows_dev // cols_count
    spread = rows_count // cols_count
    col_index = lax.axis_index("cols")
    row_place = lax.axis_index("rows")
    compact_forward_transform = fourier_matrix(rows_count, -1)
    large_forward = fourier_matrix(rows_dev, -1)
    compact_inverse_transform = fourier_matrix(rows_count, 1)
    large_inverse = fourier_matrix(rows_dev, 1)
    wave_index = jnp.arange(rows_count, dtype=jnp.int32)
    pixel_index = jnp.arange(rows_dev, dtype=jnp.int32)
    band = col_index * part_rows + jnp.arange(part_rows, dtype=jnp.int32)
    stacked_planes = jnp.stack([flow_across, downward_flow]).reshape(2, rows_dev, 1, cols_dev)
    stacked_planes = across_columns(stacked_planes).reshape(2, part_rows, rows_count, rows_dev)
    power_spectra = contract_indices("pibc,pbqk->qikc", stacked_planes, compact_forward_transform)[
        :, None
    ]
    cosine, sine_part = phase_pair(wave_index[:, None] * pixel_index[None, :], N, -1)
    power_spectra = rotate(power_spectra, cosine, sine_part)
    power_spectra = contract_indices("pfikc,pcql->qfikl", power_spectra, large_forward)
    fields = power_spectra.shape[1]
    back_cos, back_sin = phase_pair(wave_index[:, None] * pixel_index[None, :], N, 1)
    power_spectra = across_rows(power_spectra)
    power_spectra = power_spectra.reshape(2, fields, rows_count, part_rows, rows_dev)
    power_spectra = contract_indices("pfrik,prqm->qfmik", power_spectra, compact_forward_transform)
    band_cos, band_sin = phase_pair(wave_index[:, None] * band[None, :], N, -1)
    power_spectra = rotate(power_spectra, band_cos[:, :, None], band_sin[:, :, None])
    power_spectra = across_columns(
        power_spectra.reshape(2 * fields, rows_count, part_rows, rows_dev)
    )
    power_spectra = power_spectra.reshape(2, fields, spread, rows_dev, rows_dev)
    power_spectra = contract_indices("pfmsk,psql->qfmlk", power_spectra, large_forward)
    row_freq = (
        rows_count * pixel_index[None, :]
        + (col_index * spread + jnp.arange(spread, dtype=jnp.int32))[:, None]
    )
    row_wave = signed_wave(row_freq)[:, :, None]
    col_wave = signed_wave(rows_count * pixel_index + row_place)
    mixed = weigh_spectra(power_spectra, row_wave, col_wave)
    mixed = contract_indices("pmlk,plqs->qsmk", mixed, large_inverse)
    mixed = across_columns(mixed)
    band_cos, band_sin = phase_pair(band[:, None] * wave_index[None, :], N, 1)
    mixed = rotate(mixed, band_cos[:, :, None], band_sin[:, :, None])
    mixed = contract_indices("pimk,pmqr->qirk", mixed, compact_inverse_transform)
    mixed = across_rows(mixed.reshape(2, 1, part_rows, rows_count, rows_dev))
    mixed = mixed.reshape(2, rows_count, part_rows, rows_dev)
    mixed = contract_indices("pnik,pkqa->qina", mixed, large_inverse)
    mixed = rotate(mixed, back_cos, back_sin)
    image = jnp.einsum(
        "pina,pnb->iba",
        mixed,
        compact_inverse_transform[:, :, 0, :],
        precision=highest,
        preferred_element_type=jnp.float32,
    )
    image = image.reshape(part_rows, cols_count, cols_dev) * (1.0 / (N * N))
    return lax.all_to_all(image, "cols", split_axis=1, concat_axis=0, tiled=True).reshape(
        rows_dev, cols_dev
    )


def solution(mesh):
    return jax.shard_map(
        per_device,
        mesh=mesh,
        in_specs=(
            P(None, "rows", "cols"),
            P(None, "rows", "cols"),
            P(None, "rows", "cols"),
            P(None, "rows", "cols"),
            P(None, "rows", "cols"),
            P(None, "rows", "cols"),
        ),
        out_specs=P("rows", "cols"),
        check_vma=False,
    )
```

profile of v0, /device:TPU:1, one launch (start us, length us, event | category | flops | bytes accessed | tf_op | source)
XLA Modules:
  0.0 269.9 jit_solution(17173574557437066686)
XLA Ops:
  0.0 1.5 fusion.62
  1.5 5.4 %collective-permute-start = (bf16[2,8,1024]{2,1,0:T(8,128)(2,1)}, bf16[2,8,1024]{2,1,0:T(8,128)(2,1)S(1)}, u32[]{:S(2)}, u32[]{:S(2)}) collective-permute-start(bf16[2,8,1024]{2,1,0:T(8,128)(2,1)} %get-tuple-element.27), channel_id=1, source_target_pairs={{0,8},{8,16},{16,24},{24,32},{32,40},{40,48},{48,56},{56,64},{64,7... | collective-permute-start | bytes 98312 | tf_op jit(solution)/shard_map/ppermute | solution.py:26
  6.9 4.7 %collective-permute-start.1 = (bf16[2,8,1024]{2,1,0:T(8,128)(2,1)S(1)}, bf16[2,8,1024]{2,1,0:T(8,128)(2,1)S(1)}, u32[]{:S(2)}, u32[]{:S(2)}) collective-permute-start(bf16[2,8,1024]{2,1,0:T(8,128)(2,1)S(1)} %get-tuple-element.28), channel_id=1, source_target_pairs={{8,0},{16,8},{24,16},{32,24},{40,32},{48,40},{56,48},{64,56},{72,6... | collective-permute-start | bytes 98312 | tf_op jit(solution)/shard_map/ppermute | solution.py:27
  17.7 1.1 pad_maximum_fusion.1
  19.0 4.9 %copy.120 = bf16[2,1152,128]{2,0,1:T(2,128)(2,1)S(1)} copy(bf16[2,1152,128]{2,1,0:T(8,128)(2,1)S(1)} %reshape.681) | data formatting | bytes 1179648 | tf_op jit(solution)/shard_map/reshape | solution.py:73
  24.0 13.7 %gather_fusion = bf16[2048,2,128]{2,1,0:T(2,128)(2,1)} fusion(bf16[2,1152,128]{2,0,1:T(2,128)(2,1)S(1)} %copy.120, s32[2048]{0:T(1024)S(1)} %broadcast_clamp_fusion), kind=kCustom, calls=%fused_computation | custom fusion | bytes 2105344 | tf_op jit(solution)/shard_map/jit(_take)/gather | solution.py:76
  37.7 5.4 %broadcast_select_fusion = bf16[2,2,128,8,128]{4,0,3,2,1:T(2,128)(2,1)S(1)} fusion(bf16[2,2,128,8,128]{4,0,3,2,1:T(2,128)(2,1)} %bitcast.207, pred[2,128,8]{2,1,0:T(8,128)(4,1)S(1)} %copy-done.5), kind=kLoop, calls=%fused_computation.7 | loop fusion | flops 524288 | bytes 2099200 | tf_op jit(solution)/shard_map/jit(_take)/select_n | solution.py:76
  43.2 23.8 %multiply_reduce_fusion.4 = (f32[2,128,8,128]{3,0,2,1:T(2,128)S(1)}, f32[2,128,8,128]{3,0,2,1:T(2,128)S(1)}, f32[2,128,8,128]{3,0,2,1:T(2,128)S(1)}, f32[2,128,8...) fusion(f32[2,128,8]{2,1,0:T(8,128)S(1)} %copy.122, ...), kind=kLoop, calls=%fused_computation.5 | loop fusion | flops 7864320 | bytes 7389184 | tf_op jit(solution)/shard_map/reduce_sum | solution.py:85
  67.5 2.7 slice_reduce_fusion.1
  71.1 1.4 fusion.18
  72.6 1.8 copy.127
  74.4 3.6 %all-to-all-start = ((f32[2,128,1,1024]{3,0,2,1:T(2,128)}), f32[2,128,1,1024]{3,0,2,1:T(2,128)S(1)}, u32[]{:S(2)}, u32[]{:S(2)}) async-start(f32[2,128,1,1024]{3,0,2,1:T(2,128)} %copy.127), calls=%async_computation | async-start | bytes 2097152 | tf_op jit(solution)/shard_map/all_to_all | solution.py:63
  79.0 13.9 %all-to-all-done = f32[2,128,1,1024]{3,0,2,1:T(2,128)S(1)} async-done(((f32[2,128,1,1024]{3,0,2,1:T(2,128)}), f32[2,128,1,1024]{3,0,2,1:T(2,128)S(1)}, u32[]{:S(2)}, u32[]{:S(2)}) %all-to-all-start) | async-done | bytes 1048608 | tf_op jit(solution)/shard_map/all_to_all | solution.py:63
  93.7 1.1 convolution_bitcast_fusion.5
  96.0 1.6 copy.130
  97.5 14.1 %all-to-all-start.1 = ((f32[2,1,16,64,128]{4,2,0,1,3:T(8,128)}), f32[2,1,16,64,128]{4,2,0,1,3:T(8,128)S(1)}, u32[]{:S(2)}, u32[]{:S(2)}) async-start(f32[2,1,16,64,128]{4,2,0,1,3:T(8,128)} %copy.130), calls=%async_computation.1 | async-start | bytes 2097152 | tf_op jit(solution)/shard_map/all_to_all | solution.py:67
  111.8 29.6 %all-to-all-done.1 = f32[2,1,16,64,128]{4,2,0,1,3:T(8,128)S(1)} async-done(((f32[2,1,16,64,128]{4,2,0,1,3:T(8,128)}), f32[2,1,16,64,128]{4,2,0,1,3:T(8,128)S(1)}, u32[]{:S(2)}, u32[]{:S(2)}) %all-to-all-start.1) | async-done | bytes 1048608 | tf_op jit(solution)/shard_map/all_to_all | solution.py:67
  141.4 1.6 convolution_bitcast_fusion.3
  143.4 1.6 copy.132
  145.0 15.4 %all-to-all-start.2 = ((f32[2,64,16,128]{3,2,0,1:T(8,128)}), f32[2,64,16,128]{3,2,0,1:T(8,128)S(1)}, u32[]{:S(2)}, u32[]{:S(2)}) async-start(f32[2,64,16,128]{3,2,0,1:T(8,128)} %copy.132), calls=%async_computation.2 | async-start | bytes 2097152 | tf_op jit(solution)/shard_map/all_to_all | solution.py:63
  161.1 12.5 %all-to-all-done.2 = f32[2,64,16,128]{3,2,0,1:T(8,128)S(1)} async-done(((f32[2,64,16,128]{3,2,0,1:T(8,128)}), f32[2,64,16,128]{3,2,0,1:T(8,128)S(1)}, u32[]{:S(2)}, u32[]{:S(2)}) %all-to-all-start.2) | async-done | bytes 1048608 | tf_op jit(solution)/shard_map/all_to_all | solution.py:63
  173.8 1.0 fusion.21
  175.2 1.0 convolution_bitcast_fusion.2
  176.2 1.6 copy.138
  177.8 3.6 %all-to-all-start.3 = ((f32[2,128,8,128]{3,2,0,1:T(8,128)}), f32[2,128,8,128]{3,2,0,1:T(8,128)S(1)}, u32[]{:S(2)}, u32[]{:S(2)}) async-start(f32[2,128,8,128]{3,2,0,1:T(8,128)} %copy.138), calls=%async_computation.3 | async-start | bytes 2097152 | tf_op jit(solution)/shard_map/all_to_all | solution.py:63
  181.8 14.5 %all-to-all-done.3 = f32[2,128,8,128]{3,2,0,1:T(8,128)S(1)} async-done(((f32[2,128,8,128]{3,2,0,1:T(8,128)}), f32[2,128,8,128]{3,2,0,1:T(8,128)S(1)}, u32[]{:S(2)}, u32[]{:S(2)}) %all-to-all-start.3) | async-done | bytes 1048608 | tf_op jit(solution)/shard_map/all_to_all | solution.py:63
  196.8 1.1 convolution_bitcast_fusion.1
  197.9 1.6 copy.141
  199.5 14.0 %all-to-all-start.4 = ((f32[2,1,16,64,128]{4,2,0,1,3:T(8,128)}), f32[2,1,16,64,128]{4,2,0,1,3:T(8,128)S(1)}, u32[]{:S(2)}, u32[]{:S(2)}) async-start(f32[2,1,16,64,128]{4,2,0,1,3:T(8,128)} %copy.141), calls=%async_computation.4 | async-start | bytes 2097152 | tf_op jit(solution)/shard_map/all_to_all | solution.py:67
  213.6 29.8 %all-to-all-done.4 = f32[2,1,16,64,128]{4,2,0,1,3:T(8,128)S(1)} async-done(((f32[2,1,16,64,128]{4,2,0,1,3:T(8,128)}), f32[2,1,16,64,128]{4,2,0,1,3:T(8,128)S(1)}, u32[]{:S(2)}, u32[]{:S(2)}) %all-to-all-start.4) | async-done | bytes 1048608 | tf_op jit(solution)/shard_map/all_to_all | solution.py:67
  243.4 1.4 convolution_bitcast_fusion
  246.1 23.0 %all_to_all.90 = f32[16,8,1024]{2,0,1:T(8,128)S(1)} all-to-all(f32[16,8,1024]{2,0,1:T(8,128)S(1)} %copy.145), channel_id=1, replica_groups=mesh['rows'=64,'cols'=8] {'cols'}, dimensions={1} | all-to-all | bytes 1048576 | tf_op jit(solution)/shard_map/all_to_all | solution.py:164
  (70 shorter events, 15.5 us)
Async XLA Ops:
  0.0 17.4 %copy-start = (bf16[4,128,1024]{2,1,0:T(8,128)(2,1)S(1)}, bf16[4,128,1024]{2,1,0:T(8,128)(2,1)}, u32[]{:S(2)}) copy-start(bf16[4,128,1024]{2,1,0:T(8,128)(2,1)} %param.7) | copy-start | bytes 3145732
  1.5 16.2 %collective-permute-start = (bf16[2,8,1024]{2,1,0:T(8,128)(2,1)}, bf16[2,8,1024]{2,1,0:T(8,128)(2,1)S(1)}, u32[]{:S(2)}, u32[]{:S(2)}) collective-permute-start(bf16[2,8,1024]{2,1,0:T(8,128)(2,1)} %get-tuple-element.27), channel_id=1, source_target_pairs={{0,8},{8,16},{16,24},{24,32},{32,40},{40,48},{48,56},{56,64},{64,7... | collective-permute-start | bytes 98312 | tf_op jit(solution)/shard_map/ppermute | solution.py:26
  6.9 10.8 %collective-permute-start.1 = (bf16[2,8,1024]{2,1,0:T(8,128)(2,1)S(1)}, bf16[2,8,1024]{2,1,0:T(8,128)(2,1)S(1)}, u32[]{:S(2)}, u32[]{:S(2)}) collective-permute-start(bf16[2,8,1024]{2,1,0:T(8,128)(2,1)S(1)} %get-tuple-element.28), channel_id=1, source_target_pairs={{8,0},{16,8},{24,16},{32,24},{40,32},{48,40},{56,48},{64,56},{72,6... | collective-permute-start | bytes 98312 | tf_op jit(solution)/shard_map/ppermute | solution.py:27
  24.0 13.8 %copy-start.5 = (pred[2,128,8]{2,1,0:T(8,128)(4,1)S(1)}, pred[2,128,8]{2,1,0:T(8,128)(4,1)}, u32[]{:S(2)}) copy-start(pred[2,128,8]{2,1,0:T(8,128)(4,1)} %copy.118) | copy-start | bytes 6148
  24.0 19.2 %copy-start.1 = (f32[2,128,8]{2,1,0:T(8,128)S(1)}, f32[2,128,8]{2,1,0:T(8,128)}, u32[]{:S(2)}) copy-start(f32[2,128,8]{2,1,0:T(8,128)} %copy.123) | copy-start | bytes 24580
  24.0 19.2 %copy-start.2 = (f32[2,128,8]{2,1,0:T(8,128)S(1)}, f32[2,128,8]{2,1,0:T(8,128)}, u32[]{:S(2)}) copy-start(f32[2,128,8]{2,1,0:T(8,128)} %copy.124) | copy-start | bytes 24580
  24.0 19.2 %copy-start.3 = (f32[2,128,8]{2,1,0:T(8,128)S(1)}, f32[2,128,8]{2,1,0:T(8,128)}, u32[]{:S(2)}) copy-start(f32[2,128,8]{2,1,0:T(8,128)} %copy.125) | copy-start | bytes 24580
  24.0 19.2 %copy-start.4 = (f32[2,128,8]{2,1,0:T(8,128)S(1)}, f32[2,128,8]{2,1,0:T(8,128)}, u32[]{:S(2)}) copy-start(f32[2,128,8]{2,1,0:T(8,128)} %copy.126) | copy-start | bytes 24580
  74.4 18.5 %all-to-all-start = ((f32[2,128,1,1024]{3,0,2,1:T(2,128)}), f32[2,128,1,1024]{3,0,2,1:T(2,128)S(1)}, u32[]{:S(2)}, u32[]{:S(2)}) async-start(f32[2,128,1,1024]{3,0,2,1:T(2,128)} %copy.127), calls=%async_computation | async-start | bytes 2097152 | tf_op jit(solution)/shard_map/all_to_all | solution.py:63
  97.5 43.9 %all-to-all-start.1 = ((f32[2,1,16,64,128]{4,2,0,1,3:T(8,128)}), f32[2,1,16,64,128]{4,2,0,1,3:T(8,128)S(1)}, u32[]{:S(2)}, u32[]{:S(2)}) async-start(f32[2,1,16,64,128]{4,2,0,1,3:T(8,128)} %copy.130), calls=%async_computation.1 | async-start | bytes 2097152 | tf_op jit(solution)/shard_map/all_to_all | solution.py:67
  145.0 28.6 %all-to-all-start.2 = ((f32[2,64,16,128]{3,2,0,1:T(8,128)}), f32[2,64,16,128]{3,2,0,1:T(8,128)S(1)}, u32[]{:S(2)}, u32[]{:S(2)}) async-start(f32[2,64,16,128]{3,2,0,1:T(8,128)} %copy.132), calls=%async_computation.2 | async-start | bytes 2097152 | tf_op jit(solution)/shard_map/all_to_all | solution.py:63
  177.8 18.5 %all-to-all-start.3 = ((f32[2,128,8,128]{3,2,0,1:T(8,128)}), f32[2,128,8,128]{3,2,0,1:T(8,128)S(1)}, u32[]{:S(2)}, u32[]{:S(2)}) async-start(f32[2,128,8,128]{3,2,0,1:T(8,128)} %copy.138), calls=%async_computation.3 | async-start | bytes 2097152 | tf_op jit(solution)/shard_map/all_to_all | solution.py:63
  199.5 43.9 %all-to-all-start.4 = ((f32[2,1,16,64,128]{4,2,0,1,3:T(8,128)}), f32[2,1,16,64,128]{4,2,0,1,3:T(8,128)S(1)}, u32[]{:S(2)}, u32[]{:S(2)}) async-start(f32[2,1,16,64,128]{4,2,0,1,3:T(8,128)} %copy.141), calls=%async_computation.4 | async-start | bytes 2097152 | tf_op jit(solution)/shard_map/all_to_all | solution.py:67
where the time goes:
time: 273 us; the launch traced here: 270 us
  waiting for transfers between devices  100 us (37%)
  starting transfers between devices  60.6 us (22%)
  local copies, waits for them, and re-layouts  38.7 us (14%)
  other arithmetic  37.7 us (14%)
  blocking collectives  23 us (8%)
  matrix products  8.93 us (3%)
    all_to_all x2, waiting for transfers between devices, across_rows(): lax.all_to_all(values, 'rows', split_axis=3, concat_axis=1, tiled=True)  59.4 us
    all_to_all x3, waiting for transfers between devices, across_columns(): lax.all_to_all(values, 'cols', split_axis=1, concat_axis=2, tiled=True)  41 us
    all_to_all x2, starting transfers between devices, across_rows(): lax.all_to_all(values, 'rows', split_axis=3, concat_axis=1, tiled=True)  28.1 us
    reduce_sum x1, other arithmetic, remap_tiles(): pulled = pulled + jnp.sum(window * weights[None, :, :, :, None], axis=1)  23.8 us
    all_to_all x1, blocking collectives, per_device(): lax.all_to_all(image, 'cols', split_axis=1, concat_axis=0, tiled=True)  23 us
    all_to_all x3, starting transfers between devices, across_columns(): lax.all_to_all(values, 'cols', split_axis=1, concat_axis=2, tiled=True)  22.5 us
    gather x1, local copies, waits for them, and re-layouts, remap_tiles(): picked = jnp.take(tile_rows, flat_index.reshape(-1), axis=1)  13.7 us
    dot_general x7, matrix products, contract_indices(): jnp.einsum(formula, values, matrix, precision=highest, preferred_element_...  8.23 us
  transfers between devices with their start and end apart: 7, of which 5 were waited for; matrix products, arithmetic and copies ran while one was open for 3% of the time, Pallas kernels for 0%

commit v1 on v0

v1 whole, which is shorter than its diff:
```python
import functools
import math

import jax
import jax.numpy as jnp
import ml_dtypes
import numpy as np
from jax import lax
from jax.experimental import pallas as pl
from jax.experimental.pallas import tpu as pltpu
from jax.sharding import PartitionSpec as P

N = 8192
TILE = 128
HALO = 8
SHIFT = 2
LOCAL_WEIGHT = 0.5
FLOOR = 8.0 * math.pi / N

F32 = jnp.float32
BF16 = jnp.bfloat16


def split_table(x):
    hi = x.astype(ml_dtypes.bfloat16)
    lo = (x - hi.astype(np.float64)).astype(ml_dtypes.bfloat16)
    return hi, lo


def cs(angle):
    return np.cos(angle), np.sin(angle)


@functools.lru_cache(maxsize=None)
def tables():
    two_pi = 2.0 * np.pi
    t = {}
    p = np.arange(64)[None, :]
    kk = np.arange(32)[:, None]
    c, s = cs(two_pi * ((p * kk) % 64) / 64)
    d1 = np.concatenate([c, -s], 0)
    d1[32] = (-1.0) ** np.arange(64)
    t["d1"] = split_table(d1)
    d4 = np.concatenate([2 * c, -2 * s], 0).T.copy()
    d4[:, 0] = 1.0
    d4[:, 32] = (-1.0) ** np.arange(64)
    t["d4"] = split_table(d4 / (N * N))
    q = np.arange(128)[None, :]
    c, s = cs(two_pi * (kk * q) / N)
    t["tw1"] = np.stack([c, s]).astype(np.float32)
    l = np.arange(128)[:, None]
    c, s = cs(two_pi * ((l * q) % 128) / 128)
    f2 = np.block([[c, s], [-s, c]])
    t["f2"] = split_table(f2)
    t["f4"] = split_table(np.block([[c, s], [-s, c]]))
    c32, s32 = cs(two_pi * ((q * (32 + 64 * l)) % N) / N)
    low = l < 64
    alt = np.broadcast_to((-1.0) ** q, (1, 128))
    m0 = np.zeros((256, 256))
    m0[:128, :128] = np.where(low, c, 0.0)
    m0[128:, :128] = np.where(low, -s, 0.0)
    m0[128:129, :128] = alt
    m0[:128, 128:] = np.where(low, 0.0, c32)
    m0[128:, 128:] = np.where(low, 0.0, -s32)
    t["m0"] = split_table(m0)
    mi = 2.0 * m0
    mi[0] *= 0.5
    mi[128] *= 0.5
    t["m0i"] = split_table(mi)
    r = np.arange(64)[:, None]
    m = np.arange(64)[None, :]
    c, s = cs(two_pi * ((r * m) % 64) / 64)
    e_re = np.concatenate([c, s], 0)
    e_im = np.concatenate([-s, c], 0)
    t["e"] = split_table(np.concatenate([e_re, e_im, -e_im, e_re], 1))
    t["e4"] = split_table(np.block([[c, -s], [s, c]]))
    q2 = np.arange(128)[:, None]
    mm = np.concatenate([np.arange(64), np.arange(64)])[None, :]
    c, s = cs(two_pi * (q2 * mm) / N)
    t["tw2"] = np.stack([c, s]).astype(np.float32)
    n = np.arange(128)[:, None]
    c, s = cs(two_pi * ((n * q2.T) % 128) / 128)
    t["w2"] = split_table(np.concatenate([c, -s], 1))
    t["w3"] = split_table(np.block([[s, -c], [c, s]]))
    a = mm + 64 * n
    signed = np.where(a > N // 2, a - N, np.where(a == N // 2, 0, a))
    t["ka"] = (signed * (two_pi / N)).astype(np.float32)
    return t


def split(x):
    hi = x.astype(BF16)
    return hi, (x - hi.astype(F32)).astype(BF16)


def dot(a, b, transposed=False):
    dims = (((1,), (1 if transposed else 0,)), ((), ()))
    return lax.dot_general(a, b, dims, preferred_element_type=F32)


def dot3(a, b, transposed=False):
    (ah, al), (bh, bl) = a, b
    return dot(ah, bh, transposed) + (dot(ah, bl, transposed) + dot(al, bh, transposed))


def pair(ref):
    return ref[0], ref[1]


def pull_kernel(x, before, after, slopes, tile, rshift, pshift, frac, o, padded, cols):
    padded[:, 0:HALO, :] = before[...].astype(F32)
    padded[:, HALO : HALO + 128, :] = x[...].astype(F32)
    padded[:, HALO + 128 :, :] = after[...].astype(F32)
    flat = lambda ref: ref[...].reshape(16, 128)
    lane = lax.broadcasted_iota(jnp.int32, (16, 128), 1)
    index = flat(tile) * 32 + (lax.rem(lane, 16) + HALO) + flat(rshift)
    ps = flat(pshift)
    f = flat(frac)
    rows = [index.astype(F32)]
    for off in range(-SHIFT, SHIFT + 2):
        w = jnp.where(ps == off, 1.0 - f, 0.0) + jnp.where(ps + 1 == off, f, 0.0)
        rows.append(w)
    rows.append(jnp.zeros((16, 128), F32))
    cols[...] = jnp.concatenate(rows, 0).T

    spot = lax.broadcasted_iota(jnp.int32, (16, 256), 1).astype(F32)
    lane_j = lax.broadcasted_iota(jnp.int32, (16, 128), 1)

    def block(b, _):
        r0 = pl.multiple_of(b * 16, 16)
        window = [
            jnp.concatenate(
                [padded[p, pl.ds(r0, 32), u * 128 : (u + 1) * 128] for u in range(8)], 0
            )
            for p in range(2)
        ]
        window = jnp.concatenate(window, 1).astype(BF16)
        tab = cols[pl.ds(r0, 16), :]
        hot = jnp.concatenate(
            [jnp.where(tab[:, kt : kt + 1] == spot, 1.0, 0.0) for kt in range(16)], 0
        ).astype(BF16)
        picked = dot(hot, window)
        for t in range(8):
            got = []
            for p in range(2):
                total = None
                for oi in range(6):
                    off = oi - SHIFT
                    z = None
                    for k in range(2):
                        kt = k * 8 + t
                        w = tab[:, 16 * (oi + 1) + kt : 16 * (oi + 1) + kt + 1]
                        part = w * picked[kt * 16 : kt * 16 + 16, p * 128 : p * 128 + 128]
                        z = part if z is None else z + part
                    if off != 0:
                        z = pltpu.roll(z, (-off) % 128, 1)
                        keep = lane_j >= -off if off < 0 else lane_j < 128 - off
                        z = jnp.where(keep, z, 0.0)
                    total = z if total is None else total + z
                got.append(total)
            s = [slopes[i, pl.ds(r0, 16), t * 128 : (t + 1) * 128].astype(F32) for i in range(4)]
            o[b, t, 0] = -(got[0] * s[0] + got[1] * s[1])
            o[b, t, 1] = -(got[0] * s[2] + got[1] * s[3])
        return 0

    lax.fori_loop(0, 8, block, 0)


def column_kernel(g, d1, tw, f2, m0, o, ure, uim):
    cos, sin = tw[0], tw[1]
    for grp in range(8):
        x = jnp.concatenate([g[pl.ds(grp * 4 + j, 64, stride=32), :] for j in range(4)], 1)
        v = dot3(pair(d1), split(x))
        for j in range(4):
            re = v[:32, j * 128 : (j + 1) * 128]
            im = v[32:, j * 128 : (j + 1) * 128]
            ure[pl.ds(grp * 4 + j, 32, stride=32), :] = re * cos + im * sin
            uim[pl.ds(grp * 4 + j, 32, stride=32), :] = im * cos - re * sin
    lane = lax.broadcasted_iota(jnp.int32, (256, 128), 1)
    for kg in range(4):
        rows = slice(kg * 256, (kg + 1) * 256)
        rhs = split(jnp.concatenate([ure[rows, :], uim[rows, :]], 1))
        out = dot3(pair(f2), rhs, True)
        for h in range(2):
            part = out[:, h * 128 : (h + 1) * 128]
            if kg == 0 and h == 0:
                special = dot3(pair(m0), (rhs[0][:128], rhs[1][:128]), True)
                part = jnp.where(lane < 32, special, part)
            for ri in range(2):
                o[pl.ds(kg * 4 + ri * 2 + h, 128, stride=16), :] = part[ri * 128 : (ri + 1) * 128]


def row_kernel(kb, x, e, tw, w2, ka_ref, w3, e4, o, uh, ul, sh, sl, yh, yl):
    for c in range(8):
        cos = jnp.concatenate([tw[0, c * 16 : c * 16 + 16, :]] * 8, 0)
        sin = jnp.concatenate([tw[1, c * 16 : c * 16 + 16, :]] * 8, 0)
        for h in range(2):
            block = jnp.concatenate(
                [x[pl.ds(c * 4 + ri * 2 + h, 64, stride=32), :] for ri in range(2)], 0
            )
            both = dot3(split(block.T), pair(e))
            v, vs = both[:, :128], both[:, 128:]
            u = split(v * cos - vs * sin)
            us = split(vs * cos + v * sin)
            for kf in range(8):
                at = pl.ds((h * 8 + kf) * 128 + c * 16, 16)
                part = slice(kf * 16, kf * 16 + 16)
                uh[at, :] = u[0][part]
                ul[at, :] = u[1][part]
                sh[at, :] = us[0][part]
                sl[at, :] = us[1][part]
    ka = ka_ref[...]
    ka2 = ka * ka + FLOOR * FLOOR
    sign = jnp.where(lax.broadcasted_iota(jnp.int32, (128, 128), 1) < 64, -1.0, 1.0)

    def stack(first, second, col):
        parts = []
        for f in range(2):
            at = slice((col * 2 + f) * 128, (col * 2 + f + 1) * 128)
            parts.append(jnp.concatenate([first[at, :], second[at, :]], 0))
        return jnp.concatenate(parts, 1)

    for pr in range(4):
        q, qs = [], []
        for j in range(2):
            col = pr * 2 + j
            out = dot3(pair(w2), (stack(uh, sh, col), stack(ul, sl, col)))
            wb = kb[col]
            weight = LOCAL_WEIGHT + 1.0 / (ka2 + wb * wb)
            mixed = weight * (wb * out[:, :128] + ka * out[:, 128:])
            q.append(mixed)
            qs.append(pltpu.roll(mixed, 64, 1) * sign)
        rhs = jnp.concatenate([jnp.concatenate(q, 1), jnp.concatenate(qs, 1)], 0)
        back = dot3(pair(w3), split(rhs))
        for j in range(2):
            col = pr * 2 + j
            b = back[:128, j * 128 : (j + 1) * 128]
            bs = back[128:, j * 128 : (j + 1) * 128]
            y = split(b * tw[0] + bs * tw[1])
            for c in range(8):
                at = pl.ds(c * 128 + col * 16, 16)
                yh[at, :] = y[0][c * 16 : c * 16 + 16]
                yl[at, :] = y[1][c * 16 : c * 16 + 16]
    for c in range(8):
        rows = slice(c * 128, (c + 1) * 128)
        out = dot3(pair(e4), (yh[rows, :], yl[rows, :]), True)
        for ri in range(2):
            o[pl.ds(c * 2 + ri, 64, stride=16), :] = out[ri * 64 : (ri + 1) * 64]


def image_kernel(t, f4, m0i, tw, d4, o, vre, vim):
    for kg in range(4):
        block = [t[pl.ds(kg * 2 + ri, 128, stride=8), :].T for ri in range(2)]
        lhs = split(jnp.concatenate(block, 1))
        v = dot3(lhs, pair(f4))
        if kg == 0:
            special = dot3((lhs[0][:16], lhs[1][:16]), pair(m0i))
            v = jnp.concatenate([special, v[16:]], 0)
        for col in range(8):
            kk = kg * 8 + col
            re = v[col * 16 : col * 16 + 16, :128]
            im = v[col * 16 : col * 16 + 16, 128:]
            cos = tw[0, kk : kk + 1, :]
            sin = tw[1, kk : kk + 1, :]
            vre[kk * 16 : kk * 16 + 16, :] = re * cos - im * sin
            vim[kk * 16 : kk * 16 + 16, :] = im * cos + re * sin
    for grp in range(4):
        cols = []
        for j in range(4):
            at = pl.ds(grp * 4 + j, 32, stride=16)
            cols.append(jnp.concatenate([vre[at, :], vim[at, :]], 0))
        out = dot3(pair(d4), split(jnp.concatenate(cols, 1)))
        for j in range(4):
            i = grp * 4 + j
            for c in range(8):
                o[pl.ds(c * 128 + (i // 8) * 64 + i % 8, 8, stride=8), :] = out[
                    c * 8 : c * 8 + 8, j * 128 : (j + 1) * 128
                ]


def call(kernel, out_shape, scratch, *args, smem=(), **kw):
    specs = [
        pl.BlockSpec(memory_space=pltpu.SMEM if i in smem else pltpu.VMEM)
        for i in range(len(args))
    ]
    return pl.pallas_call(
        kernel,
        out_shape=jax.ShapeDtypeStruct(out_shape, F32),
        in_specs=specs,
        out_specs=pl.BlockSpec(memory_space=pltpu.VMEM),
        scratch_shapes=scratch,
        **kw,
    )(*args)


def two(table):
    return jnp.asarray(np.stack(table))


def pull(x, before, after, slopes, tile, rshift, pshift, frac):
    flip = lambda y: jnp.transpose(y, (0, 2, 1))
    return call(
        pull_kernel,
        (8, 8, 2, 16, 128),
        [pltpu.VMEM((2, 144, 1024), F32), pltpu.VMEM((128, 128), F32)],
        x, before, after, slopes, flip(tile), flip(rshift), flip(pshift), flip(frac),
    )


def column_transform(g):
    t = tables()
    return call(
        column_kernel,
        (2048, 128),
        [pltpu.VMEM((1024, 128), F32)] * 2,
        g, two(t["d1"]), jnp.asarray(t["tw1"]), two(t["f2"]), two(t["m0"]),
    )


def row_transform(x, device):
    t = tables()
    group, low = device // 4, device % 4
    kk = low * 8 + jnp.arange(8, dtype=jnp.int32)
    b = kk + 64 * group + jnp.where((kk == 0) & (group >= 64), 32, 0)
    kb = jnp.where(b > N // 2, b - N, b).astype(F32) * (2.0 * math.pi / N)
    return call(
        row_kernel,
        (1024, 128),
        [pltpu.VMEM((2048, 128), BF16)] * 4 + [pltpu.VMEM((1024, 128), BF16)] * 2,
        kb, x, two(t["e"]), jnp.asarray(t["tw2"]), two(t["w2"]), jnp.asarray(t["ka"]),
        two(t["w3"]), two(t["e4"]), smem=(0,),
    )


def image_transform(y):
    t = tables()
    return call(
        image_kernel,
        (1024, 128),
        [pltpu.VMEM((512, 128), F32)] * 2,
        y, two(t["f4"]), two(t["m0i"]), jnp.asarray(t["tw1"]), two(t["d4"]),
    )


def per_device(residual, field_slopes, source_tile, row_shift, pixel_shift, fraction):
    peers = lax.axis_size("rows")
    up = [(i, i + 1) for i in range(peers - 1)]
    down = [(j, i) for i, j in up]
    before = lax.ppermute(residual[:, -HALO:], "rows", up)
    after = lax.ppermute(residual[:, :HALO], "rows", down)
    flow = pull(
        residual, before, after, field_slopes, source_tile, row_shift, pixel_shift, fraction
    )
    flow = lax.all_to_all(flow, "cols", split_axis=0, concat_axis=0, tiled=True)
    spectra = column_transform(flow.reshape(2048, 128))
    spectra = lax.all_to_all(
        spectra.reshape(512, 4, 128), ("rows", "cols"), split_axis=0, concat_axis=0, tiled=True
    )
    device = lax.axis_index("rows") * lax.axis_size("cols") + lax.axis_index("cols")
    mixed = row_transform(spectra.reshape(2048, 128), device)
    mixed = lax.all_to_all(
        mixed.reshape(512, 2, 128), ("rows", "cols"), split_axis=0, concat_axis=0, tiled=True
    )
    image = image_transform(mixed.reshape(1024, 128))
    image = lax.all_to_all(
        image.reshape(8, 2, 8, 8, 128), "cols", split_axis=0, concat_axis=0, tiled=True
    )
    return jnp.transpose(image, (0, 1, 3, 2, 4)).reshape(128, 1024)


def solution(mesh):
    spec = P(None, "rows", "cols")
    return jax.shard_map(
        per_device,
        mesh=mesh,
        in_specs=(spec,) * 6,
        out_specs=P("rows", "cols"),
        check_vma=False,
    )
```

time: 273 us -> 163 us (0.60)
  waiting for transfers between devices: 100 us -> 33.5 us
  blocking collectives: 23 us -> 64 us
  other arithmetic: 37.7 us -> 0.58 us
  local copies, waits for them, and re-layouts: 38.7 us -> 3.15 us
  Pallas kernels: 0 us -> 32.6 us
  starting transfers between devices: 60.6 us -> 28.2 us
  matrix products: 8.93 us -> 0 us
    all_to_all x5 -> x1, waiting for transfers between devices: 100 us -> 32.4 us  [per_device(): lax.all_to_all(spectra.reshape(512, 4, 128), ('rows', 'cols'), split_axis...]
    all_to_all x1 -> x3, blocking collectives: 23 us -> 64 us  [the longest x1 33.9 us: per_device(): lax.all_to_all(mixed.reshape(512, 2, 128), ('rows', 'cols'), split_axis=0...]
    all_to_all x5 -> x1, starting transfers between devices: 50.6 us -> 17.6 us  [per_device(): lax.all_to_all(spectra.reshape(512, 4, 128), ('rows', 'cols'), split_axis...]
    pallas_call x0 -> x4, Pallas kernels: none -> 32.6 us  [call(): pl.pallas_call(kernel, out_shape=jax.ShapeDtypeStruct(out_shape, F32), in...]
    reduce_sum x1 -> x0, other arithmetic: 23.8 us -> none  [remap_tiles(): pulled = pulled + jnp.sum(window * weights[None, :, :, :, None], axis=1)]
    gather x1 -> x0, local copies, waits for them, and re-layouts: 13.7 us -> none  [remap_tiles(): picked = jnp.take(tile_rows, flat_index.reshape(-1), axis=1)]
    reshape x7 -> x0, local copies, waits for them, and re-layouts: 10.4 us -> none  [the longest x2 5.16 us: remap_tiles(): tile_rows = padded.reshape(2, (rows_dev + 2 * HALO) * tiles_dev, TILE)]
    dot_general x8 -> x0, matrix products: 8.93 us -> none  [the longest x7 8.23 us: contract_indices(): jnp.einsum(formula, values, matrix, precision=highest, preferred_element_...]
  transfers between devices with their start and end apart: 7 -> 3, of which waited for: 5 -> 2; matrix products, arithmetic and copies ran while one was open for 3% -> 0% of each run, Pallas kernels for 0% -> 0%
where the time goes in v1:
time: 163 us; the launch traced here: 162 us
  blocking collectives  64 us (39%)
  waiting for transfers between devices  33.5 us (21%)
  Pallas kernels  32.6 us (20%)
  starting transfers between devices  28.2 us (17%)
  local copies, waits for them, and re-layouts  3.15 us (2%)
    all_to_all x1, blocking collectives, per_device(): lax.all_to_all(mixed.reshape(512, 2, 128), ('rows', 'cols'), split_axis=0...  33.9 us
    pallas_call x4, Pallas kernels, call(): pl.pallas_call(kernel, out_shape=jax.ShapeDtypeStruct(out_shape, F32), in...  32.6 us
    all_to_all x1, waiting for transfers between devices, per_device(): lax.all_to_all(spectra.reshape(512, 4, 128), ('rows', 'cols'), split_axis...  32.4 us
    all_to_all x1, blocking collectives, per_device(): flow = lax.all_to_all(flow, 'cols', split_axis=0, concat_axis=0, tiled=True)  18.9 us
    all_to_all x1, starting transfers between devices, per_device(): lax.all_to_all(spectra.reshape(512, 4, 128), ('rows', 'cols'), split_axis...  17.6 us
    all_to_all x1, blocking collectives, per_device(): lax.all_to_all(image.reshape(8, 2, 8, 8, 128), 'cols', split_axis=0, conc...  11.2 us
    ppermute x1, starting transfers between devices, per_device(): after = lax.ppermute(residual[:, :HALO], 'rows', down)  8.73 us
  transfers between devices with their start and end apart: 3, of which 2 were waited for; matrix products, arithmetic and copies ran while one was open for 0% of the time, Pallas kernels for 0%

profile of v1, /device:TPU:1, one launch (start us, length us, event | category | flops | bytes accessed | tf_op | source)
XLA Modules:
  0.0 162.1 jit_solution(3104179962130725660)
XLA Ops:
  0.0 0.8 fusion.3
  0.8 8.7 %collective-permute-start.1 = (bf16[2,8,1024]{2,1,0:T(8,128)(2,1)S(1)}, bf16[2,8,1024]{2,1,0:T(8,128)(2,1)S(1)}, u32[]{:S(2)}, u32[]{:S(2)}) collective-permute-start(bf16[2,8,1024]{2,1,0:T(8,128)(2,1)S(1)} %get-tuple-element.5), channel_id=1, source_target_pairs={{8,0},{16,8},{24,16},{32,24},{40,32},{48,40},{56,48},{64,56},{72,6... | collective-permute-start | bytes 98312 | tf_op jit(solution)/shard_map/ppermute | solution.py:350
  9.5 1.9 %collective-permute-start = (bf16[2,8,1024]{2,1,0:T(8,128)(2,1)S(1)}, bf16[2,8,1024]{2,1,0:T(8,128)(2,1)S(1)}, u32[]{:S(2)}, u32[]{:S(2)}) collective-permute-start(bf16[2,8,1024]{2,1,0:T(8,128)(2,1)S(1)} %get-tuple-element.6), channel_id=1, source_target_pairs={{0,8},{8,16},{16,24},{24,32},{32,40},{40,48},{48,56},{56,64},{64,7... | collective-permute-start | bytes 98312 | tf_op jit(solution)/shard_map/ppermute | solution.py:349
  11.5 0.0 collective-permute-done.1.after
  11.5 0.0 copy-start.1
  11.5 1.2 collective-permute-done.before
  12.6 0.0 copy-start.2
  12.6 0.0 copy-done.1
  12.6 0.6 copy-done.2
  13.2 19.4 %shard_map.181 = f32[8,8,2,16,128]{4,3,2,1,0:T(8,128)} custom-call(bf16[2,128,1024]{2,1,0:T(8,128)(2,1)} %x.1, bf16[2,8,1024]{2,1,0:T(8,128)(2,1)} %copy-done.2, bf16[2,8,1024]{2,1,0:T(8,128)(2,1)} %copy-done.1, bf16[4,128,1024]{2,1,0:T(8,128)(2,1)} %slopes.1, s32[2,8,128]{2,1,0:T(8,128)} %bitcast.20, s32[2,8,128]{2,1,0:T(8,128)} %bitcast.21, ...), custom_call_target="tpu_custom_call" | custom-call | tf_op jit(solution)/shard_map/pallas_call | solution.py:286
  32.6 18.9 %all_to_all.20 = f32[8,8,2,16,128]{4,3,2,1,0:T(8,128)} all-to-all(f32[8,8,2,16,128]{4,3,2,1,0:T(8,128)} %shard_map.181), channel_id=1, replica_groups=mesh['rows'=64,'cols'=8] {'cols'}, dimensions={0} | all-to-all | bytes 2097152 | tf_op jit(solution)/shard_map/all_to_all | solution.py:354
  51.5 4.8 %shard_map.182 = f32[2048,128]{1,0:T(8,128)} custom-call(f32[2048,128]{1,0:T(8,128)} %bitcast.15, bf16[2,64,64]{2,1,0:T(8,128)(2,1)} %constant.74.clone.d1, f32[2,32,128]{2,1,0:T(8,128)} %constant.75.clone.tw, bf16[2,256,256]{2,1,0:T(8,128)(2,1)} %constant.76.clone.f2.f4, bf16[2,256,256]{2,1,0:T(8,128)(2,1)} %constant.77.clone.m0), custom_call_target="tpu_custom_call" | custom-call | tf_op jit(solution)/shard_map/pallas_call | solution.py:286
  56.3 17.6 %all-to-all-start.1 = ((f32[512,4,128]{2,1,0:T(4,128)}), f32[512,4,128]{2,1,0:T(4,128)S(1)}, u32[]{:S(2)}, u32[]{:S(2)}) async-start(f32[512,4,128]{2,1,0:T(4,128)} %bitcast.14), calls=%async_computation.1 | async-start | bytes 2097152 | tf_op jit(solution)/shard_map/all_to_all | solution.py:356
  73.9 0.6 fusion.2.kb
  74.5 32.4 %all-to-all-done.1 = f32[512,4,128]{2,1,0:T(4,128)S(1)} async-done(((f32[512,4,128]{2,1,0:T(4,128)}), f32[512,4,128]{2,1,0:T(4,128)S(1)}, u32[]{:S(2)}, u32[]{:S(2)}) %all-to-all-start.1) | async-done | bytes 1048608 | tf_op jit(solution)/shard_map/all_to_all | solution.py:356
  106.8 0.0 copy-start
  106.8 1.0 copy-done
  107.8 5.5 %shard_map.183 = f32[1024,128]{1,0:T(8,128)} custom-call(f32[8]{0:T(128)} %fusion.2.kb, f32[2048,128]{1,0:T(8,128)} %bitcast.13, bf16[2,128,256]{2,1,0:T(8,128)(2,1)} %constant.78.clone.e, f32[2,128,128]{2,1,0:T(8,128)} %constant.79.clone.tw, bf16[2,128,256]{2,1,0:T(8,128)(2,1)} %constant.80.clone.w2, f32[128,128]{1,0:T(8,128)} %constant.81.clone.ka_ref, ...), custom_call_target="tpu_custom_call" | custom-call | tf_op jit(solution)/shard_map/pallas_call | solution.py:286
  113.3 33.9 %all_to_all.21 = f32[512,2,128]{2,1,0:T(2,128)} all-to-all(f32[512,2,128]{2,1,0:T(2,128)} %bitcast.16), channel_id=1, replica_groups=mesh['rows'=64,'cols'=8] {'rows','cols'}, dimensions={0} | all-to-all | bytes 1048576 | tf_op jit(solution)/shard_map/all_to_all | solution.py:361
  147.1 2.9 %shard_map.184 = f32[1024,128]{1,0:T(8,128)} custom-call(f32[1024,128]{1,0:T(8,128)} %bitcast.17, bf16[2,256,256]{2,1,0:T(8,128)(2,1)} %constant.76.clone.f2.f4, bf16[2,256,256]{2,1,0:T(8,128)(2,1)} %constant.84.clone.m0i, f32[2,32,128]{2,1,0:T(8,128)} %constant.75.clone.tw, bf16[2,64,64]{2,1,0:T(8,128)(2,1)} %constant.85.clone.d4), custom_call_target="tpu_custom_call" | custom-call | tf_op jit(solution)/shard_map/pallas_call | solution.py:286
  150.1 11.2 %all_to_all.22 = f32[8,2,8,8,128]{4,3,2,1,0:T(8,128)S(1)} all-to-all(f32[8,2,8,8,128]{4,3,2,1,0:T(8,128)} %bitcast.18), channel_id=1, replica_groups=mesh['rows'=64,'cols'=8] {'cols'}, dimensions={0} | all-to-all | bytes 1048576 | tf_op jit(solution)/shard_map/all_to_all | solution.py:365
  161.3 0.8 copy.21
Async XLA Ops:
  0.8 10.7 %collective-permute-start.1 = (bf16[2,8,1024]{2,1,0:T(8,128)(2,1)S(1)}, bf16[2,8,1024]{2,1,0:T(8,128)(2,1)S(1)}, u32[]{:S(2)}, u32[]{:S(2)}) collective-permute-start(bf16[2,8,1024]{2,1,0:T(8,128)(2,1)S(1)} %get-tuple-element.5), channel_id=1, source_target_pairs={{8,0},{16,8},{24,16},{32,24},{40,32},{48,40},{56,48},{64,56},{72,6... | collective-permute-start | bytes 98312 | tf_op jit(solution)/shard_map/ppermute | solution.py:350
  9.5 3.1 %collective-permute-start = (bf16[2,8,1024]{2,1,0:T(8,128)(2,1)S(1)}, bf16[2,8,1024]{2,1,0:T(8,128)(2,1)S(1)}, u32[]{:S(2)}, u32[]{:S(2)}) collective-permute-start(bf16[2,8,1024]{2,1,0:T(8,128)(2,1)S(1)} %get-tuple-element.6), channel_id=1, source_target_pairs={{0,8},{8,16},{16,24},{24,32},{32,40},{40,48},{48,56},{56,64},{64,7... | collective-permute-start | bytes 98312 | tf_op jit(solution)/shard_map/ppermute | solution.py:349
  11.5 1.2 copy-start.1
  12.6 0.6 copy-start.2
  56.3 50.5 %all-to-all-start.1 = ((f32[512,4,128]{2,1,0:T(4,128)}), f32[512,4,128]{2,1,0:T(4,128)S(1)}, u32[]{:S(2)}, u32[]{:S(2)}) async-start(f32[512,4,128]{2,1,0:T(4,128)} %bitcast.14), calls=%async_computation.1 | async-start | bytes 2097152 | tf_op jit(solution)/shard_map/all_to_all | solution.py:356
  106.8 1.0 copy-start

commit v2 on v1

--- a/solution.py
+++ b/solution.py
@@ -107,24 +107,34 @@
     return ref[0], ref[1]
 
 
-def pull_kernel(x, before, after, slopes, tile, rshift, pshift, frac, o, padded, cols):
+def pull_kernel(x, before, after, slopes, tile, rshift, pshift, frac, o, padded, spots, wts, sc):
     padded[:, 0:HALO, :] = before[...].astype(F32)
     padded[:, HALO : HALO + 128, :] = x[...].astype(F32)
     padded[:, HALO + 128 :, :] = after[...].astype(F32)
-    flat = lambda ref: ref[...].reshape(16, 128)
-    lane = lax.broadcasted_iota(jnp.int32, (16, 128), 1)
-    index = flat(tile) * 32 + (lax.rem(lane, 16) + HALO) + flat(rshift)
-    ps = flat(pshift)
-    f = flat(frac)
-    rows = [index.astype(F32)]
-    for off in range(-SHIFT, SHIFT + 2):
-        w = jnp.where(ps == off, 1.0 - f, 0.0) + jnp.where(ps + 1 == off, f, 0.0)
-        rows.append(w)
-    rows.append(jnp.zeros((16, 128), F32))
-    cols[...] = jnp.concatenate(rows, 0).T
-
-    spot = lax.broadcasted_iota(jnp.int32, (16, 256), 1).astype(F32)
-    lane_j = lax.broadcasted_iota(jnp.int32, (16, 128), 1)
+    sc[:, :, 0:8, :] = jnp.zeros((2, 2, 8, 128), F32)
+    sc[:, :, 136:144, :] = jnp.zeros((2, 2, 8, 128), F32)
+    lane = lax.broadcasted_iota(jnp.int32, (8, 128), 1)
+
+    def by_block(values):
+        out = jnp.zeros((8, 128), values.dtype)
+        for t in range(8):
+            row = jnp.broadcast_to(values[t : t + 1, :], (8, 128))
+            row = pltpu.roll(pltpu.roll(row, (16 * t + 16) % 128, 1), 0, 1, stride=16, stride_axis=0)
+            out = jnp.where((lane >= 16 * t) & (lane < 16 * t + 16), row, out)
+        return out
+
+    for k in range(2):
+        rows = slice(k * 8, k * 8 + 8)
+        index = tile[k] * 32 + (lax.rem(lane, 16) + HALO) + rshift[k]
+        spots[rows, :] = by_block(index)
+        ps = by_block(pshift[k])
+        f = by_block(frac[k])
+        for oi in range(6):
+            off = oi - SHIFT
+            wts[oi, rows, :] = jnp.where(ps == off, 1.0 - f, 0.0) + jnp.where(
+                ps + 1 == off, f, 0.0
+            )
+    place = lax.broadcasted_iota(jnp.int32, (256, 128), 0)
 
     def block(b, _):
         r0 = pl.multiple_of(b * 16, 16)
@@ -135,32 +145,34 @@
             for p in range(2)
         ]
         window = jnp.concatenate(window, 1).astype(BF16)
-        tab = cols[pl.ds(r0, 16), :]
         hot = jnp.concatenate(
-            [jnp.where(tab[:, kt : kt + 1] == spot, 1.0, 0.0) for kt in range(16)], 0
-        ).astype(BF16)
-        picked = dot(hot, window)
+            [
+                jnp.where(place == spots[pl.ds(k * 8 + 7 - b, 1), :], 1.0, 0.0).astype(BF16)
+                for k in range(2)
+            ],
+            1,
+        )
+        picked = lax.dot_general(
+            window, hot, (((0,), (0,)), ((), ())), preferred_element_type=F32
+        )
+        for p in range(2):
+            for k in range(2):
+                sc[p, k, 8:136, :] = picked[p * 128 : p * 128 + 128, k * 128 : k * 128 + 128]
+        got = []
+        for p in range(2):
+            total = None
+            for oi in range(6):
+                for k in range(2):
+                    w = wts[oi, pl.ds(k * 8 + 7 - b, 1), :]
+                    part = w * sc[p, k, 8 + oi - SHIFT : 136 + oi - SHIFT, :]
+                    total = part if total is None else total + part
+            got.append(total.T)
         for t in range(8):
-            got = []
-            for p in range(2):
-                total = None
-                for oi in range(6):
-                    off = oi - SHIFT
-                    z = None
-                    for k in range(2):
-                        kt = k * 8 + t
-                        w = tab[:, 16 * (oi + 1) + kt : 16 * (oi + 1) + kt + 1]
-                        part = w * picked[kt * 16 : kt * 16 + 16, p * 128 : p * 128 + 128]
-                        z = part if z is None else z + part
-                    if off != 0:
-                        z = pltpu.roll(z, (-off) % 128, 1)
-                        keep = lane_j >= -off if off < 0 else lane_j < 128 - off
-                        z = jnp.where(keep, z, 0.0)
-                    total = z if total is None else total + z
-                got.append(total)
+            at = slice(t * 16, t * 16 + 16)
+            first, second = got[0][at], got[1][at]
             s = [slopes[i, pl.ds(r0, 16), t * 128 : (t + 1) * 128].astype(F32) for i in range(4)]
-            o[b, t, 0] = -(got[0] * s[0] + got[1] * s[1])
-            o[b, t, 1] = -(got[0] * s[2] + got[1] * s[3])
+            o[b, t, 0] = -(first * s[0] + second * s[1])
+            o[b, t, 1] = -(first * s[2] + second * s[3])
         return 0
 
     lax.fori_loop(0, 8, block, 0)
@@ -302,7 +314,12 @@
     return call(
         pull_kernel,
         (8, 8, 2, 16, 128),
-        [pltpu.VMEM((2, 144, 1024), F32), pltpu.VMEM((128, 128), F32)],
+        [
+            pltpu.VMEM((2, 144, 1024), F32),
+            pltpu.VMEM((16, 128), jnp.int32),
+            pltpu.VMEM((6, 16, 128), F32),
+            pltpu.VMEM((2, 2, 144, 128), F32),
+        ],
         x, before, after, slopes, flip(tile), flip(rshift), flip(pshift), flip(frac),
     )
 

time: 163 us -> 150 us (0.920)
  Pallas kernels: 32.6 us -> 18.9 us
    pallas_call x4, Pallas kernels: 32.6 us -> 18.9 us  [call(): pl.pallas_call(kernel, out_shape=jax.ShapeDtypeStruct(out_shape, F32), in...]
where the time goes in v2:
time: 150 us; the launch traced here: 148 us
  blocking collectives  64 us (43%)
  waiting for transfers between devices  33.5 us (22%)
  starting transfers between devices  28.2 us (19%)
  Pallas kernels  18.9 us (13%)
  local copies, waits for them, and re-layouts  3.15 us (2%)
    all_to_all x1, blocking collectives, per_device(): lax.all_to_all(mixed.reshape(512, 2, 128), ('rows', 'cols'), split_axis=0...  33.9 us
    all_to_all x1, waiting for transfers between devices, per_device(): lax.all_to_all(spectra.reshape(512, 4, 128), ('rows', 'cols'), split_axis...  32.4 us
    pallas_call x4, Pallas kernels, call(): pl.pallas_call(kernel, out_shape=jax.ShapeDtypeStruct(out_shape, F32), in...  18.9 us
    all_to_all x1, blocking collectives, per_device(): flow = lax.all_to_all(flow, 'cols', split_axis=0, concat_axis=0, tiled=True)  18.9 us
    all_to_all x1, starting transfers between devices, per_device(): lax.all_to_all(spectra.reshape(512, 4, 128), ('rows', 'cols'), split_axis...  17.6 us
    all_to_all x1, blocking collectives, per_device(): lax.all_to_all(image.reshape(8, 2, 8, 8, 128), 'cols', split_axis=0, conc...  11.2 us
    ppermute x1, starting transfers between devices, per_device(): after = lax.ppermute(residual[:, :HALO], 'rows', down)  8.73 us
  transfers between devices with their start and end apart: 3, of which 2 were waited for; matrix products, arithmetic and copies ran while one was open for 0% of the time, Pallas kernels for 0%

profile of v2, /device:TPU:1, one launch (start us, length us, event | category | flops | bytes accessed | tf_op | source)
XLA Modules:
  0.0 148.4 jit_solution(243002520294684609)
XLA Ops:
  0.0 0.8 fusion.3
  0.8 8.7 %collective-permute-start.1 = (bf16[2,8,1024]{2,1,0:T(8,128)(2,1)S(1)}, bf16[2,8,1024]{2,1,0:T(8,128)(2,1)S(1)}, u32[]{:S(2)}, u32[]{:S(2)}) collective-permute-start(bf16[2,8,1024]{2,1,0:T(8,128)(2,1)S(1)} %get-tuple-element.5), channel_id=1, source_target_pairs={{8,0},{16,8},{24,16},{32,24},{40,32},{48,40},{56,48},{64,56},{72,6... | collective-permute-start | bytes 98312 | tf_op jit(solution)/shard_map/ppermute | solution.py:367
  9.5 1.9 %collective-permute-start = (bf16[2,8,1024]{2,1,0:T(8,128)(2,1)S(1)}, bf16[2,8,1024]{2,1,0:T(8,128)(2,1)S(1)}, u32[]{:S(2)}, u32[]{:S(2)}) collective-permute-start(bf16[2,8,1024]{2,1,0:T(8,128)(2,1)S(1)} %get-tuple-element.6), channel_id=1, source_target_pairs={{0,8},{8,16},{16,24},{24,32},{32,40},{40,48},{48,56},{56,64},{64,7... | collective-permute-start | bytes 98312 | tf_op jit(solution)/shard_map/ppermute | solution.py:366
  11.5 0.0 collective-permute-done.1.after
  11.5 0.0 copy-start.1
  11.5 1.2 collective-permute-done.before
  12.6 0.0 copy-start.2
  12.6 0.0 copy-done.1
  12.6 0.6 copy-done.2
  13.2 5.7 %shard_map.181 = f32[8,8,2,16,128]{4,3,2,1,0:T(8,128)} custom-call(bf16[2,128,1024]{2,1,0:T(8,128)(2,1)} %x.1, bf16[2,8,1024]{2,1,0:T(8,128)(2,1)} %copy-done.2, bf16[2,8,1024]{2,1,0:T(8,128)(2,1)} %copy-done.1, bf16[4,128,1024]{2,1,0:T(8,128)(2,1)} %slopes.1, s32[2,8,128]{2,1,0:T(8,128)} %bitcast.20, s32[2,8,128]{2,1,0:T(8,128)} %bitcast.21, ...), custom_call_target="tpu_custom_call" | custom-call | tf_op jit(solution)/shard_map/pallas_call | solution.py:298
  19.0 18.9 %all_to_all.20 = f32[8,8,2,16,128]{4,3,2,1,0:T(8,128)} all-to-all(f32[8,8,2,16,128]{4,3,2,1,0:T(8,128)} %shard_map.181), channel_id=1, replica_groups=mesh['rows'=64,'cols'=8] {'cols'}, dimensions={0} | all-to-all | bytes 2097152 | tf_op jit(solution)/shard_map/all_to_all | solution.py:371
  37.8 4.8 %shard_map.182 = f32[2048,128]{1,0:T(8,128)} custom-call(f32[2048,128]{1,0:T(8,128)} %bitcast.15, bf16[2,64,64]{2,1,0:T(8,128)(2,1)} %constant.74.clone.d1, f32[2,32,128]{2,1,0:T(8,128)} %constant.75.clone.tw, bf16[2,256,256]{2,1,0:T(8,128)(2,1)} %constant.76.clone.f2.f4, bf16[2,256,256]{2,1,0:T(8,128)(2,1)} %constant.77.clone.m0), custom_call_target="tpu_custom_call" | custom-call | tf_op jit(solution)/shard_map/pallas_call | solution.py:298
  42.6 17.6 %all-to-all-start.1 = ((f32[512,4,128]{2,1,0:T(4,128)}), f32[512,4,128]{2,1,0:T(4,128)S(1)}, u32[]{:S(2)}, u32[]{:S(2)}) async-start(f32[512,4,128]{2,1,0:T(4,128)} %bitcast.14), calls=%async_computation.1 | async-start | bytes 2097152 | tf_op jit(solution)/shard_map/all_to_all | solution.py:373
  60.2 0.6 fusion.2.kb
  60.8 32.4 %all-to-all-done.1 = f32[512,4,128]{2,1,0:T(4,128)S(1)} async-done(((f32[512,4,128]{2,1,0:T(4,128)}), f32[512,4,128]{2,1,0:T(4,128)S(1)}, u32[]{:S(2)}, u32[]{:S(2)}) %all-to-all-start.1) | async-done | bytes 1048608 | tf_op jit(solution)/shard_map/all_to_all | solution.py:373
  93.1 0.0 copy-start
  93.2 1.0 copy-done
  94.1 5.5 %shard_map.183 = f32[1024,128]{1,0:T(8,128)} custom-call(f32[8]{0:T(128)} %fusion.2.kb, f32[2048,128]{1,0:T(8,128)} %bitcast.13, bf16[2,128,256]{2,1,0:T(8,128)(2,1)} %constant.78.clone.e, f32[2,128,128]{2,1,0:T(8,128)} %constant.79.clone.tw, bf16[2,128,256]{2,1,0:T(8,128)(2,1)} %constant.80.clone.w2, f32[128,128]{1,0:T(8,128)} %constant.81.clone.ka_ref, ...), custom_call_target="tpu_custom_call" | custom-call | tf_op jit(solution)/shard_map/pallas_call | solution.py:298
  99.6 33.9 %all_to_all.21 = f32[512,2,128]{2,1,0:T(2,128)} all-to-all(f32[512,2,128]{2,1,0:T(2,128)} %bitcast.16), channel_id=1, replica_groups=mesh['rows'=64,'cols'=8] {'rows','cols'}, dimensions={0} | all-to-all | bytes 1048576 | tf_op jit(solution)/shard_map/all_to_all | solution.py:378
  133.5 2.9 %shard_map.184 = f32[1024,128]{1,0:T(8,128)} custom-call(f32[1024,128]{1,0:T(8,128)} %bitcast.17, bf16[2,256,256]{2,1,0:T(8,128)(2,1)} %constant.76.clone.f2.f4, bf16[2,256,256]{2,1,0:T(8,128)(2,1)} %constant.84.clone.m0i, f32[2,32,128]{2,1,0:T(8,128)} %constant.75.clone.tw, bf16[2,64,64]{2,1,0:T(8,128)(2,1)} %constant.85.clone.d4), custom_call_target="tpu_custom_call" | custom-call | tf_op jit(solution)/shard_map/pallas_call | solution.py:298
  136.4 11.2 %all_to_all.22 = f32[8,2,8,8,128]{4,3,2,1,0:T(8,128)S(1)} all-to-all(f32[8,2,8,8,128]{4,3,2,1,0:T(8,128)} %bitcast.18), channel_id=1, replica_groups=mesh['rows'=64,'cols'=8] {'cols'}, dimensions={0} | all-to-all | bytes 1048576 | tf_op jit(solution)/shard_map/all_to_all | solution.py:382
  147.6 0.8 copy.21
Async XLA Ops:
  0.8 10.7 %collective-permute-start.1 = (bf16[2,8,1024]{2,1,0:T(8,128)(2,1)S(1)}, bf16[2,8,1024]{2,1,0:T(8,128)(2,1)S(1)}, u32[]{:S(2)}, u32[]{:S(2)}) collective-permute-start(bf16[2,8,1024]{2,1,0:T(8,128)(2,1)S(1)} %get-tuple-element.5), channel_id=1, source_target_pairs={{8,0},{16,8},{24,16},{32,24},{40,32},{48,40},{56,48},{64,56},{72,6... | collective-permute-start | bytes 98312 | tf_op jit(solution)/shard_map/ppermute | solution.py:367
  9.5 3.1 %collective-permute-start = (bf16[2,8,1024]{2,1,0:T(8,128)(2,1)S(1)}, bf16[2,8,1024]{2,1,0:T(8,128)(2,1)S(1)}, u32[]{:S(2)}, u32[]{:S(2)}) collective-permute-start(bf16[2,8,1024]{2,1,0:T(8,128)(2,1)S(1)} %get-tuple-element.6), channel_id=1, source_target_pairs={{0,8},{8,16},{16,24},{24,32},{32,40},{40,48},{48,56},{56,64},{64,7... | collective-permute-start | bytes 98312 | tf_op jit(solution)/shard_map/ppermute | solution.py:366
  11.5 1.2 copy-start.1
  12.6 0.6 copy-start.2
  42.6 50.5 %all-to-all-start.1 = ((f32[512,4,128]{2,1,0:T(4,128)}), f32[512,4,128]{2,1,0:T(4,128)S(1)}, u32[]{:S(2)}, u32[]{:S(2)}) async-start(f32[512,4,128]{2,1,0:T(4,128)} %bitcast.14), calls=%async_computation.1 | async-start | bytes 2097152 | tf_op jit(solution)/shard_map/all_to_all | solution.py:373
  93.1 1.0 copy-start

commit v3 on v2

--- a/solution.py
+++ b/solution.py
@@ -19,6 +19,10 @@
 
 F32 = jnp.float32
 BF16 = jnp.bfloat16
+TINY = 1e-18
+BIAS = 120.0
+STEPS = 16380.0
+CENTRE = 16384.0
 
 
 def split_table(x):
@@ -107,6 +111,38 @@
     return ref[0], ref[1]
 
 
+def spread(x, join):
+    x = join(x, pltpu.roll(x, 64, 1))
+    return join(x, pltpu.roll(x, 32, 1))
+
+
+def lane_field(shape):
+    return lax.shift_left(
+        lax.shift_right_logical(lax.broadcasted_iota(jnp.int32, shape, 1), 5), 1
+    )
+
+
+def encode(x, y):
+    peak = spread(jnp.maximum(jnp.abs(x), jnp.abs(y)), jnp.maximum)
+    level = jnp.ceil(2.0 * jnp.log2(jnp.maximum(peak, TINY))) + BIAS
+    level = jnp.clip(level, 0.0, 255.0)
+    gain = jnp.exp2((BIAS - level) * 0.5) * STEPS
+    code = level.astype(jnp.int32)
+    bits = lax.shift_right_logical(code, lane_field(x.shape)) & 3
+    qx = (x * gain + (CENTRE + 0.5)).astype(jnp.int32)
+    qy = (y * gain + (CENTRE + 0.5)).astype(jnp.int32)
+    return qx | lax.shift_left(qy, 15) | lax.shift_left(bits, 30)
+
+
+def decode(word):
+    bits = lax.shift_right_logical(word, 30) & 3
+    code = spread(lax.shift_left(bits, lane_field(word.shape)), jnp.add)
+    scale = jnp.exp2((code.astype(F32) - BIAS) * 0.5) * (1.0 / STEPS)
+    x = (word & 32767).astype(F32) - CENTRE
+    y = (lax.shift_right_logical(word, 15) & 32767).astype(F32) - CENTRE
+    return x * scale, y * scale
+
+
 def pull_kernel(x, before, after, slopes, tile, rshift, pshift, frac, o, padded, spots, wts, sc):
     padded[:, 0:HALO, :] = before[...].astype(F32)
     padded[:, HALO : HALO + 128, :] = x[...].astype(F32)
@@ -198,8 +234,7 @@
             if kg == 0 and h == 0:
                 special = dot3(pair(m0), (rhs[0][:128], rhs[1][:128]), True)
                 part = jnp.where(lane < 32, special, part)
-            for ri in range(2):
-                o[pl.ds(kg * 4 + ri * 2 + h, 128, stride=16), :] = part[ri * 128 : (ri + 1) * 128]
+            o[pl.ds(kg * 2 + h, 128, stride=8), :] = encode(part[:128], part[128:])
 
 
 def row_kernel(kb, x, e, tw, w2, ka_ref, w3, e4, o, uh, ul, sh, sl, yh, yl):
@@ -207,9 +242,7 @@
         cos = jnp.concatenate([tw[0, c * 16 : c * 16 + 16, :]] * 8, 0)
         sin = jnp.concatenate([tw[1, c * 16 : c * 16 + 16, :]] * 8, 0)
         for h in range(2):
-            block = jnp.concatenate(
-                [x[pl.ds(c * 4 + ri * 2 + h, 64, stride=32), :] for ri in range(2)], 0
-            )
+            block = jnp.concatenate(decode(x[pl.ds(c * 2 + h, 64, stride=16), :]), 0)
             both = dot3(split(block.T), pair(e))
             v, vs = both[:, :128], both[:, 128:]
             u = split(v * cos - vs * sin)
@@ -256,14 +289,13 @@
     for c in range(8):
         rows = slice(c * 128, (c + 1) * 128)
         out = dot3(pair(e4), (yh[rows, :], yl[rows, :]), True)
-        for ri in range(2):
-            o[pl.ds(c * 2 + ri, 64, stride=16), :] = out[ri * 64 : (ri + 1) * 64]
+        o[pl.ds(c, 64, stride=8), :] = encode(out[:64], out[64:])
 
 
 def image_kernel(t, f4, m0i, tw, d4, o, vre, vim):
     for kg in range(4):
-        block = [t[pl.ds(kg * 2 + ri, 128, stride=8), :].T for ri in range(2)]
-        lhs = split(jnp.concatenate(block, 1))
+        block = decode(t[pl.ds(kg, 128, stride=4), :])
+        lhs = split(jnp.concatenate([part.T for part in block], 1))
         v = dot3(lhs, pair(f4))
         if kg == 0:
             special = dot3((lhs[0][:16], lhs[1][:16]), pair(m0i))
@@ -290,14 +322,14 @@
                 ]
 
 
-def call(kernel, out_shape, scratch, *args, smem=(), **kw):
+def call(kernel, out_shape, scratch, *args, smem=(), dtype=F32, **kw):
     specs = [
         pl.BlockSpec(memory_space=pltpu.SMEM if i in smem else pltpu.VMEM)
         for i in range(len(args))
     ]
     return pl.pallas_call(
         kernel,
-        out_shape=jax.ShapeDtypeStruct(out_shape, F32),
+        out_shape=jax.ShapeDtypeStruct(out_shape, dtype),
         in_specs=specs,
         out_specs=pl.BlockSpec(memory_space=pltpu.VMEM),
         scratch_shapes=scratch,
@@ -328,9 +360,10 @@
     t = tables()
     return call(
         column_kernel,
-        (2048, 128),
+        (1024, 128),
         [pltpu.VMEM((1024, 128), F32)] * 2,
         g, two(t["d1"]), jnp.asarray(t["tw1"]), two(t["f2"]), two(t["m0"]),
+        dtype=jnp.int32,
     )
 
 
@@ -342,10 +375,10 @@
     kb = jnp.where(b > N // 2, b - N, b).astype(F32) * (2.0 * math.pi / N)
     return call(
         row_kernel,
-        (1024, 128),
+        (512, 128),
         [pltpu.VMEM((2048, 128), BF16)] * 4 + [pltpu.VMEM((1024, 128), BF16)] * 2,
         kb, x, two(t["e"]), jnp.asarray(t["tw2"]), two(t["w2"]), jnp.asarray(t["ka"]),
-        two(t["w3"]), two(t["e4"]), smem=(0,),
+        two(t["w3"]), two(t["e4"]), smem=(0,), dtype=jnp.int32,
     )
 
 
@@ -371,14 +404,14 @@
     flow = lax.all_to_all(flow, "cols", split_axis=0, concat_axis=0, tiled=True)
     spectra = column_transform(flow.reshape(2048, 128))
     spectra = lax.all_to_all(
-        spectra.reshape(512, 4, 128), ("rows", "cols"), split_axis=0, concat_axis=0, tiled=True
+        spectra.reshape(512, 2, 128), ("rows", "cols"), split_axis=0, concat_axis=0, tiled=True
     )
     device = lax.axis_index("rows") * lax.axis_size("cols") + lax.axis_index("cols")
-    mixed = row_transform(spectra.reshape(2048, 128), device)
+    mixed = row_transform(spectra.reshape(1024, 128), device)
     mixed = lax.all_to_all(
-        mixed.reshape(512, 2, 128), ("rows", "cols"), split_axis=0, concat_axis=0, tiled=True
-    )
-    image = image_transform(mixed.reshape(1024, 128))
+        mixed.reshape(512, 1, 128), ("rows", "cols"), split_axis=0, concat_axis=0, tiled=True
+    )
+    image = image_transform(mixed.reshape(512, 128))
     image = lax.all_to_all(
         image.reshape(8, 2, 8, 8, 128), "cols", split_axis=0, concat_axis=0, tiled=True
     )

time: 150 us -> 135 us (0.900)
  waiting for transfers between devices: 33.5 us -> 22.4 us
  blocking collectives: 64 us -> 59.9 us
    all_to_all x1, waiting for transfers between devices: 32.4 us -> 21.2 us  [per_device(): lax.all_to_all(spectra.reshape(512, 2, 128), ('rows', 'cols'), split_axis...]
    all_to_all x1, blocking collectives: 33.9 us -> 29.4 us  [per_device(): lax.all_to_all(mixed.reshape(512, 1, 128), ('rows', 'cols'), split_axis=0...]
where the time goes in v3:
time: 135 us; the launch traced here: 134 us
  blocking collectives  59.9 us (44%)
  starting transfers between devices  28.2 us (21%)
  waiting for transfers between devices  22.4 us (17%)
  Pallas kernels  19.8 us (15%)
  local copies, waits for them, and re-layouts  2.98 us (2%)
    all_to_all x1, blocking collectives, per_device(): lax.all_to_all(mixed.reshape(512, 1, 128), ('rows', 'cols'), split_axis=0...  29.4 us
    all_to_all x1, waiting for transfers between devices, per_device(): lax.all_to_all(spectra.reshape(512, 2, 128), ('rows', 'cols'), split_axis...  21.2 us
    pallas_call x4, Pallas kernels, call(): pl.pallas_call(kernel, out_shape=jax.ShapeDtypeStruct(out_shape, dtype),...  19.8 us
    all_to_all x1, blocking collectives, per_device(): flow = lax.all_to_all(flow, 'cols', split_axis=0, concat_axis=0, tiled=True)  18.9 us
    all_to_all x1, starting transfers between devices, per_device(): lax.all_to_all(spectra.reshape(512, 2, 128), ('rows', 'cols'), split_axis...  17.6 us
    all_to_all x1, blocking collectives, per_device(): lax.all_to_all(image.reshape(8, 2, 8, 8, 128), 'cols', split_axis=0, conc...  11.7 us
    ppermute x1, starting transfers between devices, per_device(): after = lax.ppermute(residual[:, :HALO], 'rows', down)  8.73 us
  transfers between devices with their start and end apart: 3, of which 2 were waited for; matrix products, arithmetic and copies ran while one was open for 0% of the time, Pallas kernels for 0%

profile of v3, /device:TPU:1, one launch (start us, length us, event | category | flops | bytes accessed | tf_op | source)
XLA Modules:
  0.0 134.0 jit_solution(12522096791397816606)
XLA Ops:
  0.0 0.8 fusion.3
  0.8 8.7 %collective-permute-start.1 = (bf16[2,8,1024]{2,1,0:T(8,128)(2,1)S(1)}, bf16[2,8,1024]{2,1,0:T(8,128)(2,1)S(1)}, u32[]{:S(2)}, u32[]{:S(2)}) collective-permute-start(bf16[2,8,1024]{2,1,0:T(8,128)(2,1)S(1)} %get-tuple-element.5), channel_id=1, source_target_pairs={{8,0},{16,8},{24,16},{32,24},{40,32},{48,40},{56,48},{64,56},{72,6... | collective-permute-start | bytes 98312 | tf_op jit(solution)/shard_map/ppermute | solution.py:400
  9.5 1.9 %collective-permute-start = (bf16[2,8,1024]{2,1,0:T(8,128)(2,1)S(1)}, bf16[2,8,1024]{2,1,0:T(8,128)(2,1)S(1)}, u32[]{:S(2)}, u32[]{:S(2)}) collective-permute-start(bf16[2,8,1024]{2,1,0:T(8,128)(2,1)S(1)} %get-tuple-element.6), channel_id=1, source_target_pairs={{0,8},{8,16},{16,24},{24,32},{32,40},{40,48},{48,56},{56,64},{64,7... | collective-permute-start | bytes 98312 | tf_op jit(solution)/shard_map/ppermute | solution.py:399
  11.5 0.0 collective-permute-done.1.after
  11.5 0.0 copy-start.1
  11.5 1.2 collective-permute-done.before
  12.6 0.0 copy-start.2
  12.6 0.0 copy-done.1
  12.6 0.6 copy-done.2
  13.2 5.7 %shard_map.181 = f32[8,8,2,16,128]{4,3,2,1,0:T(8,128)} custom-call(bf16[2,128,1024]{2,1,0:T(8,128)(2,1)} %x.1, bf16[2,8,1024]{2,1,0:T(8,128)(2,1)} %copy-done.2, bf16[2,8,1024]{2,1,0:T(8,128)(2,1)} %copy-done.1, bf16[4,128,1024]{2,1,0:T(8,128)(2,1)} %slopes.1, s32[2,8,128]{2,1,0:T(8,128)} %bitcast.22, s32[2,8,128]{2,1,0:T(8,128)} %bitcast.23, ...), custom_call_target="tpu_custom_call" | custom-call | tf_op jit(solution)/shard_map/pallas_call | solution.py:330
  19.0 18.9 %all_to_all.20 = f32[8,8,2,16,128]{4,3,2,1,0:T(8,128)} all-to-all(f32[8,8,2,16,128]{4,3,2,1,0:T(8,128)} %shard_map.181), channel_id=1, replica_groups=mesh['rows'=64,'cols'=8] {'cols'}, dimensions={0} | all-to-all | bytes 2097152 | tf_op jit(solution)/shard_map/all_to_all | solution.py:404
  37.8 5.0 %shard_map.182 = s32[1024,128]{1,0:T(8,128)} custom-call(f32[2048,128]{1,0:T(8,128)} %bitcast.15, bf16[2,64,64]{2,1,0:T(8,128)(2,1)} %constant.74.clone.d1, f32[2,32,128]{2,1,0:T(8,128)} %constant.75.clone.tw, bf16[2,256,256]{2,1,0:T(8,128)(2,1)} %constant.76.clone.f2.f4, bf16[2,256,256]{2,1,0:T(8,128)(2,1)} %constant.77.clone.m0), custom_call_target="tpu_custom_call" | custom-call | tf_op jit(solution)/shard_map/pallas_call | solution.py:330
  42.8 17.6 %all-to-all-start.1 = ((s32[512,2,128]{2,1,0:T(2,128)}), s32[512,2,128]{2,1,0:T(2,128)S(1)}, u32[]{:S(2)}, u32[]{:S(2)}) async-start(s32[512,2,128]{2,1,0:T(2,128)} %bitcast.19), calls=%async_computation.1 | async-start | bytes 1048576 | tf_op jit(solution)/shard_map/all_to_all | solution.py:406
  60.4 0.6 fusion.2.kb
  61.0 21.2 %all-to-all-done.1 = s32[512,2,128]{2,1,0:T(2,128)S(1)} async-done(((s32[512,2,128]{2,1,0:T(2,128)}), s32[512,2,128]{2,1,0:T(2,128)S(1)}, u32[]{:S(2)}, u32[]{:S(2)}) %all-to-all-start.1) | async-done | bytes 524320 | tf_op jit(solution)/shard_map/all_to_all | solution.py:406
  82.2 0.0 copy-start
  82.2 0.8 copy-done
  83.0 5.9 %shard_map.183 = s32[512,128]{1,0:T(8,128)} custom-call(f32[8]{0:T(128)} %fusion.2.kb, s32[1024,128]{1,0:T(8,128)} %bitcast.16, bf16[2,128,256]{2,1,0:T(8,128)(2,1)} %constant.78.clone.e, f32[2,128,128]{2,1,0:T(8,128)} %constant.79.clone.tw, bf16[2,128,256]{2,1,0:T(8,128)(2,1)} %constant.80.clone.w2, f32[128,128]{1,0:T(8,128)} %constant.81.clone.ka_ref, ...), custom_call_target="tpu_custom_call" | custom-call | tf_op jit(solution)/shard_map/pallas_call | solution.py:330
  89.0 29.4 %all_to_all.21 = s32[512,1,128]{2,1,0:T(1,128)} all-to-all(s32[512,1,128]{2,1,0:T(1,128)} %bitcast.20), channel_id=1, replica_groups=mesh['rows'=64,'cols'=8] {'rows','cols'}, dimensions={0} | all-to-all | bytes 524288 | tf_op jit(solution)/shard_map/all_to_all | solution.py:411
  118.4 3.2 %shard_map.184 = f32[1024,128]{1,0:T(8,128)} custom-call(s32[512,128]{1,0:T(8,128)} %bitcast.21, bf16[2,256,256]{2,1,0:T(8,128)(2,1)} %constant.76.clone.f2.f4, bf16[2,256,256]{2,1,0:T(8,128)(2,1)} %constant.84.clone.m0i, f32[2,32,128]{2,1,0:T(8,128)} %constant.75.clone.tw, bf16[2,64,64]{2,1,0:T(8,128)(2,1)} %constant.85.clone.d4), custom_call_target="tpu_custom_call" | custom-call | tf_op jit(solution)/shard_map/pallas_call | solution.py:330
  121.6 11.7 %all_to_all.22 = f32[8,2,8,8,128]{4,3,2,1,0:T(8,128)S(1)} all-to-all(f32[8,2,8,8,128]{4,3,2,1,0:T(8,128)} %bitcast.17), channel_id=1, replica_groups=mesh['rows'=64,'cols'=8] {'cols'}, dimensions={0} | all-to-all | bytes 1048576 | tf_op jit(solution)/shard_map/all_to_all | solution.py:415
  133.2 0.8 copy.22
Async XLA Ops:
  0.8 10.7 %collective-permute-start.1 = (bf16[2,8,1024]{2,1,0:T(8,128)(2,1)S(1)}, bf16[2,8,1024]{2,1,0:T(8,128)(2,1)S(1)}, u32[]{:S(2)}, u32[]{:S(2)}) collective-permute-start(bf16[2,8,1024]{2,1,0:T(8,128)(2,1)S(1)} %get-tuple-element.5), channel_id=1, source_target_pairs={{8,0},{16,8},{24,16},{32,24},{40,32},{48,40},{56,48},{64,56},{72,6... | collective-permute-start | bytes 98312 | tf_op jit(solution)/shard_map/ppermute | solution.py:400
  9.5 3.1 %collective-permute-start = (bf16[2,8,1024]{2,1,0:T(8,128)(2,1)S(1)}, bf16[2,8,1024]{2,1,0:T(8,128)(2,1)S(1)}, u32[]{:S(2)}, u32[]{:S(2)}) collective-permute-start(bf16[2,8,1024]{2,1,0:T(8,128)(2,1)S(1)} %get-tuple-element.6), channel_id=1, source_target_pairs={{0,8},{8,16},{16,24},{24,32},{32,40},{40,48},{48,56},{56,64},{64,7... | collective-permute-start | bytes 98312 | tf_op jit(solution)/shard_map/ppermute | solution.py:399
  11.5 1.2 copy-start.1
  12.6 0.6 copy-start.2
  42.8 39.4 %all-to-all-start.1 = ((s32[512,2,128]{2,1,0:T(2,128)}), s32[512,2,128]{2,1,0:T(2,128)S(1)}, u32[]{:S(2)}, u32[]{:S(2)}) async-start(s32[512,2,128]{2,1,0:T(2,128)} %bitcast.19), calls=%async_computation.1 | async-start | bytes 1048576 | tf_op jit(solution)/shard_map/all_to_all | solution.py:406
  82.2 0.8 copy-start

commit v4 on v3

--- a/solution.py
+++ b/solution.py
@@ -55,7 +55,9 @@
     l = np.arange(128)[:, None]
     c, s = cs(two_pi * ((l * q) % 128) / 128)
     f2 = np.block([[c, s], [-s, c]])
-    t["f2"] = split_table(f2)
+    order = np.concatenate([np.arange(0, 128, 2), np.arange(1, 128, 2)])
+    order = np.concatenate([order, 128 + order])
+    t["f2"] = split_table(f2[order])
     t["f4"] = split_table(np.block([[c, s], [-s, c]]))
     c32, s32 = cs(two_pi * ((q * (32 + 64 * l)) % N) / N)
     low = l < 64
@@ -66,7 +68,7 @@
     m0[128:129, :128] = alt
     m0[:128, 128:] = np.where(low, 0.0, c32)
     m0[128:, 128:] = np.where(low, 0.0, -s32)
-    t["m0"] = split_table(m0)
+    t["m0"] = split_table(m0[order])
     mi = 2.0 * m0
     mi[0] *= 0.5
     mi[128] *= 0.5
@@ -111,6 +113,75 @@
     return ref[0], ref[1]
 
 
+MESH = pl.DeviceIdType.MESH
+ROWS, COLS = 64, 8
+
+
+def here():
+    return lax.axis_index("rows"), lax.axis_index("cols")
+
+
+def greet(rows):
+    r, c = here()
+    barrier = pltpu.get_barrier_semaphore()
+    for i in range(1, COLS):
+        peer = (r, lax.rem(c + i, COLS))
+        pl.semaphore_signal(barrier, inc=1, device_id=peer, device_id_type=MESH)
+    if rows:
+
+        def signal(i, _):
+            peer = (lax.rem(r + i, ROWS), c)
+            pl.semaphore_signal(barrier, inc=1, device_id=peer, device_id_type=MESH)
+            return 0
+
+        lax.fori_loop(1, ROWS, signal, 0)
+
+
+def gather(rows):
+    count = COLS - 1 + (ROWS - 1 if rows else 0)
+    pl.semaphore_wait(pltpu.get_barrier_semaphore(), count)
+
+
+def to_col(peer, src, dst, sems):
+    r, c = here()
+
+    @pl.when(peer != c)
+    def _():
+        pltpu.make_async_remote_copy(
+            src_ref=src.at[peer],
+            dst_ref=dst.at[c],
+            send_sem=sems[0],
+            recv_sem=sems[1],
+            device_id=(r, peer),
+            device_id_type=MESH,
+        ).start()
+
+
+def finish(ref, count, sem):
+    part = ref.at[pl.ds(0, count)]
+    pltpu.make_async_copy(part, part, sem).wait()
+
+
+def to_rows(src, dst, sems):
+    r, c = here()
+
+    def send(i, _):
+        peer = lax.rem(r + i, ROWS)
+        pltpu.make_async_remote_copy(
+            src_ref=src.at[:, peer],
+            dst_ref=dst.at[r],
+            send_sem=sems[0],
+            recv_sem=sems[1],
+            device_id=(peer, c),
+            device_id_type=MESH,
+        ).start()
+        return 0
+
+    lax.fori_loop(1, ROWS, send, 0)
+    dst[r] = src[:, r]
+    finish(dst, ROWS - 1, sems[1])
+
+
 def spread(x, join):
     x = join(x, pltpu.roll(x, 64, 1))
     return join(x, pltpu.roll(x, 32, 1))
@@ -143,7 +214,10 @@
     return x * scale, y * scale
 
 
-def pull_kernel(x, before, after, slopes, tile, rshift, pshift, frac, o, padded, spots, wts, sc):
+def pull_kernel(net, x, before, after, slopes, tile, rshift, pshift, frac, o, s1, padded, spots, wts, sc, *sems):
+    own = here()[1] if net else 0
+    if net:
+        greet(False)
     padded[:, 0:HALO, :] = before[...].astype(F32)
     padded[:, HALO : HALO + 128, :] = x[...].astype(F32)
     padded[:, HALO + 128 :, :] = after[...].astype(F32)
@@ -172,7 +246,8 @@
             )
     place = lax.broadcasted_iota(jnp.int32, (256, 128), 0)
 
-    def block(b, _):
+    def block(n, _):
+        b = lax.rem(own + 1 + n, COLS)
         r0 = pl.multiple_of(b * 16, 16)
         window = [
             jnp.concatenate(
@@ -207,24 +282,55 @@
             at = slice(t * 16, t * 16 + 16)
             first, second = got[0][at], got[1][at]
             s = [slopes[i, pl.ds(r0, 16), t * 128 : (t + 1) * 128].astype(F32) for i in range(4)]
-            o[b, t, 0] = -(first * s[0] + second * s[1])
-            o[b, t, 1] = -(first * s[2] + second * s[3])
+            across = -(first * s[0] + second * s[1])
+            down = -(first * s[2] + second * s[3])
+            s1[b, t * 16 : t * 16 + 16, :] = encode(across, down)
+        if net:
+
+            @pl.when(n == 1)
+            def _():
+                gather(False)
+
+            @pl.when(n > 0)
+            def _():
+                to_col(lax.rem(own + n, COLS), s1, o, sems)
+
         return 0
 
     lax.fori_loop(0, 8, block, 0)
-
-
-def column_kernel(g, d1, tw, f2, m0, o, ure, uim):
+    if net:
+        o[own] = s1[own]
+        finish(o, COLS - 1, sems[1])
+        finish(s1, COLS - 1, sems[0])
+    else:
+        o[...] = s1[...]
+
+
+def column_kernel(net, g, d1, tw, f2, m0, o, s1, r1, ure, uim, *sems):
+    if net:
+        greet(True)
+    flat = s1.reshape(1024, 128) if net else s1
     cos, sin = tw[0], tw[1]
     for grp in range(8):
-        x = jnp.concatenate([g[pl.ds(grp * 4 + j, 64, stride=32), :] for j in range(4)], 1)
-        v = dot3(pair(d1), split(x))
+        x, at = [], []
+        for i in (2 * grp, 2 * grp + 1):
+            x += decode(g[pl.ds(i, 64, stride=16), :])
+            at += [i, 16 + i]
+        v = dot3(pair(d1), split(jnp.concatenate(x, 1)))
         for j in range(4):
             re = v[:32, j * 128 : (j + 1) * 128]
             im = v[32:, j * 128 : (j + 1) * 128]
-            ure[pl.ds(grp * 4 + j, 32, stride=32), :] = re * cos + im * sin
-            uim[pl.ds(grp * 4 + j, 32, stride=32), :] = im * cos - re * sin
+            ure[pl.ds(at[j], 32, stride=32), :] = re * cos + im * sin
+            uim[pl.ds(at[j], 32, stride=32), :] = im * cos - re * sin
     lane = lax.broadcasted_iota(jnp.int32, (256, 128), 1)
+
+    def send(kg):
+        if net and kg >= 0:
+            if kg == 0:
+                gather(True)
+            to_col(kg, s1, r1, sems[:2])
+            to_col(kg + 4, s1, r1, sems[:2])
+
     for kg in range(4):
         rows = slice(kg * 256, (kg + 1) * 256)
         rhs = split(jnp.concatenate([ure[rows, :], uim[rows, :]], 1))
@@ -234,10 +340,27 @@
             if kg == 0 and h == 0:
                 special = dot3(pair(m0), (rhs[0][:128], rhs[1][:128]), True)
                 part = jnp.where(lane < 32, special, part)
-            o[pl.ds(kg * 2 + h, 128, stride=8), :] = encode(part[:128], part[128:])
-
-
-def row_kernel(kb, x, e, tw, w2, ka_ref, w3, e4, o, uh, ul, sh, sl, yh, yl):
+            word = encode(part[:128], part[128:])
+            for half in range(2):
+                at = pl.ds((half * 4 + kg) * 128 + h, 64, stride=2)
+                flat[at, :] = word[half * 64 : half * 64 + 64]
+        send(kg - 1)
+    send(3)
+    if net:
+        own = here()[1]
+        r1[own] = s1[own]
+        finish(r1, COLS - 1, sems[1])
+        to_rows(r1, o, sems[2:])
+        finish(s1, COLS - 1, sems[0])
+        finish(o, ROWS - 1, sems[2])
+    else:
+        o[...] = s1[...]
+
+
+def row_kernel(net, kb, x, e, tw, w2, ka_ref, w3, e4, o, s1, r1, uh, ul, sh, sl, yh, yl, *sems):
+    if net:
+        greet(True)
+    flat = s1.reshape(512, 128) if net else s1
     for c in range(8):
         cos = jnp.concatenate([tw[0, c * 16 : c * 16 + 16, :]] * 8, 0)
         sin = jnp.concatenate([tw[1, c * 16 : c * 16 + 16, :]] * 8, 0)
@@ -289,10 +412,27 @@
     for c in range(8):
         rows = slice(c * 128, (c + 1) * 128)
         out = dot3(pair(e4), (yh[rows, :], yl[rows, :]), True)
-        o[pl.ds(c, 64, stride=8), :] = encode(out[:64], out[64:])
-
-
-def image_kernel(t, f4, m0i, tw, d4, o, vre, vim):
+        flat[c * 64 : c * 64 + 64, :] = encode(out[:64], out[64:])
+        if net and c == 1:
+            gather(True)
+        if net and c > 0:
+            to_col(c - 1, s1, r1, sems[:2])
+    if net:
+        to_col(COLS - 1, s1, r1, sems[:2])
+        own = here()[1]
+        r1[own] = s1[own]
+        finish(r1, COLS - 1, sems[1])
+        to_rows(r1, o, sems[2:])
+        finish(s1, COLS - 1, sems[0])
+        finish(o, ROWS - 1, sems[2])
+    else:
+        o[...] = s1[...]
+
+
+def image_kernel(net, t, f4, m0i, tw, d4, o, s1, r1, vre, vim, *sems):
+    if net:
+        greet(False)
+    flat = s1.reshape(512, 128) if net else s1
     for kg in range(4):
         block = decode(t[pl.ds(kg, 128, stride=4), :])
         lhs = split(jnp.concatenate([part.T for part in block], 1))
@@ -309,31 +449,50 @@
             vre[kk * 16 : kk * 16 + 16, :] = re * cos - im * sin
             vim[kk * 16 : kk * 16 + 16, :] = im * cos + re * sin
     for grp in range(4):
+        picks = (grp * 2, grp * 2 + 8, grp * 2 + 1, grp * 2 + 9)
         cols = []
-        for j in range(4):
-            at = pl.ds(grp * 4 + j, 32, stride=16)
+        for i in picks:
+            at = pl.ds(i, 32, stride=16)
             cols.append(jnp.concatenate([vre[at, :], vim[at, :]], 0))
         out = dot3(pair(d4), split(jnp.concatenate(cols, 1)))
-        for j in range(4):
-            i = grp * 4 + j
-            for c in range(8):
-                o[pl.ds(c * 128 + (i // 8) * 64 + i % 8, 8, stride=8), :] = out[
-                    c * 8 : c * 8 + 8, j * 128 : (j + 1) * 128
-                ]
-
-
-def call(kernel, out_shape, scratch, *args, smem=(), dtype=F32, **kw):
+        for j in range(2):
+            word = encode(out[:, j * 256 : j * 256 + 128], out[:, j * 256 + 128 : j * 256 + 256])
+            flat[pl.ds(grp * 2 + j, 64, stride=8), :] = word
+    if net:
+        gather(False)
+        own = here()[1]
+        for i in range(1, COLS):
+            to_col(lax.rem(own + i, COLS), s1, r1, sems)
+        r1[own] = s1[own]
+        finish(r1, COLS - 1, sems[1])
+    else:
+        r1[...] = s1[...]
+    for c in range(8):
+        halves = decode(r1[c] if net else r1[c * 64 : c * 64 + 64, :])
+        for it in range(2):
+            for ph in range(8):
+                at = slice(c * 16 + it * 8, c * 16 + it * 8 + 8)
+                o[at, ph * 128 : ph * 128 + 128] = halves[it][ph * 8 : ph * 8 + 8]
+    if net:
+        finish(s1, COLS - 1, sems[0])
+
+
+def call(kernel, out, scratch, *args, net=None, phases=1, smem=()):
     specs = [
         pl.BlockSpec(memory_space=pltpu.SMEM if i in smem else pltpu.VMEM)
         for i in range(len(args))
     ]
+    params = {}
+    if net is not None:
+        scratch = scratch + [pltpu.SemaphoreType.DMA] * (2 * phases)
+        params["compiler_params"] = pltpu.CompilerParams(collective_id=net, has_side_effects=True)
     return pl.pallas_call(
-        kernel,
-        out_shape=jax.ShapeDtypeStruct(out_shape, dtype),
+        functools.partial(kernel, net is not None),
+        out_shape=jax.ShapeDtypeStruct(*out),
         in_specs=specs,
         out_specs=pl.BlockSpec(memory_space=pltpu.VMEM),
         scratch_shapes=scratch,
-        **kw,
+        **params,
     )(*args)
 
 
@@ -341,33 +500,39 @@
     return jnp.asarray(np.stack(table))
 
 
-def pull(x, before, after, slopes, tile, rshift, pshift, frac):
+def words(*shape):
+    return pltpu.VMEM(shape, jnp.int32)
+
+
+def pull(x, before, after, slopes, tile, rshift, pshift, frac, net=None):
     flip = lambda y: jnp.transpose(y, (0, 2, 1))
     return call(
         pull_kernel,
-        (8, 8, 2, 16, 128),
+        ((8, 128, 128), jnp.int32),
         [
+            words(8, 128, 128),
             pltpu.VMEM((2, 144, 1024), F32),
             pltpu.VMEM((16, 128), jnp.int32),
             pltpu.VMEM((6, 16, 128), F32),
             pltpu.VMEM((2, 2, 144, 128), F32),
         ],
         x, before, after, slopes, flip(tile), flip(rshift), flip(pshift), flip(frac),
-    )
-
-
-def column_transform(g):
+        net=net,
+    )
+
+
+def column_transform(g, net=None):
     t = tables()
     return call(
         column_kernel,
-        (1024, 128),
-        [pltpu.VMEM((1024, 128), F32)] * 2,
+        ((64, 8, 2, 128) if net is not None else (1024, 128), jnp.int32),
+        [words(8, 64, 2, 128) if net is not None else words(1024, 128)] * 2 + [pltpu.VMEM((1024, 128), F32)] * 2,
         g, two(t["d1"]), jnp.asarray(t["tw1"]), two(t["f2"]), two(t["m0"]),
-        dtype=jnp.int32,
-    )
-
-
-def row_transform(x, device):
+        net=net, phases=2,
+    )
+
+
+def row_transform(x, device, net=None):
     t = tables()
     group, low = device // 4, device % 4
     kk = low * 8 + jnp.arange(8, dtype=jnp.int32)
@@ -375,20 +540,24 @@
     kb = jnp.where(b > N // 2, b - N, b).astype(F32) * (2.0 * math.pi / N)
     return call(
         row_kernel,
-        (512, 128),
-        [pltpu.VMEM((2048, 128), BF16)] * 4 + [pltpu.VMEM((1024, 128), BF16)] * 2,
+        ((64, 8, 1, 128) if net is not None else (512, 128), jnp.int32),
+        [words(8, 64, 1, 128) if net is not None else words(512, 128)] * 2
+        + [pltpu.VMEM((2048, 128), BF16)] * 4
+        + [pltpu.VMEM((1024, 128), BF16)] * 2,
         kb, x, two(t["e"]), jnp.asarray(t["tw2"]), two(t["w2"]), jnp.asarray(t["ka"]),
-        two(t["w3"]), two(t["e4"]), smem=(0,), dtype=jnp.int32,
-    )
-
-
-def image_transform(y):
+        two(t["w3"]), two(t["e4"]),
+        smem=(0,), net=net, phases=2,
+    )
+
+
+def image_transform(y, net=None):
     t = tables()
     return call(
         image_kernel,
-        (1024, 128),
-        [pltpu.VMEM((512, 128), F32)] * 2,
+        ((128, 1024), F32),
+        [words(8, 64, 128) if net is not None else words(512, 128)] * 2 + [pltpu.VMEM((512, 128), F32)] * 2,
         y, two(t["f4"]), two(t["m0i"]), jnp.asarray(t["tw1"]), two(t["d4"]),
+        net=net,
     )
 
 
@@ -399,23 +568,13 @@
     before = lax.ppermute(residual[:, -HALO:], "rows", up)
     after = lax.ppermute(residual[:, :HALO], "rows", down)
     flow = pull(
-        residual, before, after, field_slopes, source_tile, row_shift, pixel_shift, fraction
-    )
-    flow = lax.all_to_all(flow, "cols", split_axis=0, concat_axis=0, tiled=True)
-    spectra = column_transform(flow.reshape(2048, 128))
-    spectra = lax.all_to_all(
-        spectra.reshape(512, 2, 128), ("rows", "cols"), split_axis=0, concat_axis=0, tiled=True
-    )
+        residual, before, after, field_slopes, source_tile, row_shift, pixel_shift, fraction,
+        net=0,
+    )
+    spectra = column_transform(flow.reshape(1024, 128), net=1)
     device = lax.axis_index("rows") * lax.axis_size("cols") + lax.axis_index("cols")
-    mixed = row_transform(spectra.reshape(1024, 128), device)
-    mixed = lax.all_to_all(
-        mixed.reshape(512, 1, 128), ("rows", "cols"), split_axis=0, concat_axis=0, tiled=True
-    )
-    image = image_transform(mixed.reshape(512, 128))
-    image = lax.all_to_all(
-        image.reshape(8, 2, 8, 8, 128), "cols", split_axis=0, concat_axis=0, tiled=True
-    )
-    return jnp.transpose(image, (0, 1, 3, 2, 4)).reshape(128, 1024)
+    mixed = row_transform(spectra.reshape(1024, 128), device, net=2)
+    return image_transform(mixed.reshape(512, 128), net=3)
 
 
 def solution(mesh):

time: 135 us -> 109 us (0.81)
  Pallas kernels: 19.8 us -> 93.2 us
  blocking collectives: 59.9 us -> 0 us
  waiting for transfers between devices: 22.4 us -> 0.55 us
  starting transfers between devices: 28.2 us -> 10.7 us
    pallas_call x4, Pallas kernels: 19.8 us -> 93.2 us  [call(): pl.pallas_call(functools.partial(kernel, net is not None), out_shape=jax....]
    all_to_all x3 -> x0, blocking collectives: 59.9 us -> none  [the longest x1 29.4 us: per_device(): lax.all_to_all(mixed.reshape(512, 1, 128), ('rows', 'cols'), split_axis=0...]
    all_to_all x1 -> x0, waiting for transfers between devices: 21.2 us -> none  [per_device(): lax.all_to_all(spectra.reshape(512, 2, 128), ('rows', 'cols'), split_axis...]
    all_to_all x1 -> x0, starting transfers between devices: 17.6 us -> none  [per_device(): lax.all_to_all(spectra.reshape(512, 2, 128), ('rows', 'cols'), split_axis...]
  transfers between devices with their start and end apart: 3 -> 2, of which waited for: 2 -> 1; matrix products, arithmetic and copies ran while one was open for 0% -> 1% of each run, Pallas kernels for 0% -> 0%
where the time goes in v4:
time: 109 us; the launch traced here: 108 us
  Pallas kernels  93.2 us (86%)
  starting transfers between devices  10.7 us (10%)
  local copies, waits for them, and re-layouts  3.28 us (3%)
    pallas_call x4, Pallas kernels, call(): pl.pallas_call(functools.partial(kernel, net is not None), out_shape=jax....  93.2 us
    ppermute x1, starting transfers between devices, per_device(): after = lax.ppermute(residual[:, :HALO], 'rows', down)  8.73 us
    unnamed x5, local copies, waits for them, and re-layouts  2.5 us
  transfers between devices with their start and end apart: 2, of which 1 were waited for; matrix products, arithmetic and copies ran while one was open for 1% of the time, Pallas kernels for 0%

profile of v4, /device:TPU:1, one launch (start us, length us, event | category | flops | bytes accessed | tf_op | source)
XLA Modules:
  0.0 108.3 jit_solution(14452142902158417403)
XLA Ops:
  0.0 0.8 fusion.3
  0.8 8.7 %collective-permute-start.1 = (bf16[2,8,1024]{2,1,0:T(8,128)(2,1)S(1)}, bf16[2,8,1024]{2,1,0:T(8,128)(2,1)S(1)}, u32[]{:S(2)}, u32[]{:S(2)}) collective-permute-start(bf16[2,8,1024]{2,1,0:T(8,128)(2,1)S(1)} %get-tuple-element.5), channel_id=1, source_target_pairs={{8,0},{16,8},{24,16},{32,24},{40,32},{48,40},{56,48},{64,56},{72,6... | collective-permute-start | bytes 98312 | tf_op jit(solution)/shard_map/ppermute | solution.py:569
  9.5 1.9 %collective-permute-start = (bf16[2,8,1024]{2,1,0:T(8,128)(2,1)S(1)}, bf16[2,8,1024]{2,1,0:T(8,128)(2,1)S(1)}, u32[]{:S(2)}, u32[]{:S(2)}) collective-permute-start(bf16[2,8,1024]{2,1,0:T(8,128)(2,1)S(1)} %get-tuple-element.6), channel_id=1, source_target_pairs={{0,8},{8,16},{16,24},{24,32},{32,40},{40,48},{48,56},{56,64},{64,7... | collective-permute-start | bytes 98312 | tf_op jit(solution)/shard_map/ppermute | solution.py:568
  11.5 0.6 fusion.2.kb
  12.1 0.0 collective-permute-done.1.after
  12.1 0.0 copy-start
  12.1 0.6 collective-permute-done.before
  12.6 0.0 copy-start.1
  12.6 0.1 copy-done
  12.7 0.6 copy-done.1
  13.2 13.3 %shard_map.181 = s32[8,128,128]{2,1,0:T(8,128)} custom-call(bf16[2,128,1024]{2,1,0:T(8,128)(2,1)} %x.1, bf16[2,8,1024]{2,1,0:T(8,128)(2,1)} %copy-done.1, bf16[2,8,1024]{2,1,0:T(8,128)(2,1)} %copy-done, bf16[4,128,1024]{2,1,0:T(8,128)(2,1)} %slopes.1, s32[2,8,128]{2,1,0:T(8,128)} %bitcast.10, s32[2,8,128]{2,1,0:T(8,128)} %bitcast.11, s32[2,8,128]{2,1,0:T(8,128)} %bitcast.12, ...), custom_call_target="tpu_custom_call" | custom-call | tf_op jit(solution)/shard_map/pallas_call | solution.py:489
  26.6 45.1 %shard_map.182 = s32[64,8,2,128]{3,2,1,0:T(2,128)} custom-call(s32[1024,128]{1,0:T(8,128)} %bitcast.8, bf16[2,64,64]{2,1,0:T(8,128)(2,1)} %constant.76.clone.d1, f32[2,32,128]{2,1,0:T(8,128)} %constant.77.clone.tw, bf16[2,256,256]{2,1,0:T(8,128)(2,1)} %constant.78.clone.f2, bf16[2,256,256]{2,1,0:T(8,128)(2,1)} %constant.79.clone.m0), custom_call_target="tpu_custom_call" | custom-call | tf_op jit(solution)/shard_map/pallas_call | solution.py:489
  71.7 22.8 %shard_map.183 = s32[64,8,1,128]{3,2,1,0:T(1,128)} custom-call(f32[8]{0:T(128)} %fusion.2.kb, s32[1024,128]{1,0:T(8,128)} %bitcast.7, bf16[2,128,256]{2,1,0:T(8,128)(2,1)} %constant.80.clone.e, f32[2,128,128]{2,1,0:T(8,128)} %constant.81.clone.tw, bf16[2,128,256]{2,1,0:T(8,128)(2,1)} %constant.82.clone.w2, f32[128,128]{1,0:T(8,128)} %constant.83.clone.ka_ref, ...), custom_call_target="tpu_custom_call" | custom-call | tf_op jit(solution)/shard_map/pallas_call | solution.py:489
  94.5 12.0 %shard_map.184 = f32[128,1024]{1,0:T(8,128)} custom-call(s32[512,128]{1,0:T(8,128)} %bitcast.9, bf16[2,256,256]{2,1,0:T(8,128)(2,1)} %constant.86.clone.f4, bf16[2,256,256]{2,1,0:T(8,128)(2,1)} %constant.87.clone.m0i, f32[2,32,128]{2,1,0:T(8,128)} %constant.77.clone.tw, bf16[2,64,64]{2,1,0:T(8,128)(2,1)} %constant.88.clone.d4), custom_call_target="tpu_custom_call" | custom-call | tf_op jit(solution)/shard_map/pallas_call | solution.py:489
  106.5 1.9 %copy.21 = f32[128,1024]{1,0:T(8,128)} copy(f32[128,1024]{1,0:T(8,128)} %shard_map.184) | data formatting | bytes 1048576
Async XLA Ops:
  0.8 11.3 %collective-permute-start.1 = (bf16[2,8,1024]{2,1,0:T(8,128)(2,1)S(1)}, bf16[2,8,1024]{2,1,0:T(8,128)(2,1)S(1)}, u32[]{:S(2)}, u32[]{:S(2)}) collective-permute-start(bf16[2,8,1024]{2,1,0:T(8,128)(2,1)S(1)} %get-tuple-element.5), channel_id=1, source_target_pairs={{8,0},{16,8},{24,16},{32,24},{40,32},{48,40},{56,48},{64,56},{72,6... | collective-permute-start | bytes 98312 | tf_op jit(solution)/shard_map/ppermute | solution.py:569
  9.5 3.1 %collective-permute-start = (bf16[2,8,1024]{2,1,0:T(8,128)(2,1)S(1)}, bf16[2,8,1024]{2,1,0:T(8,128)(2,1)S(1)}, u32[]{:S(2)}, u32[]{:S(2)}) collective-permute-start(bf16[2,8,1024]{2,1,0:T(8,128)(2,1)S(1)} %get-tuple-element.6), channel_id=1, source_target_pairs={{0,8},{8,16},{16,24},{24,32},{32,40},{40,48},{48,56},{56,64},{64,7... | collective-permute-start | bytes 98312 | tf_op jit(solution)/shard_map/ppermute | solution.py:568
  12.1 0.6 copy-start
  12.6 0.6 copy-start.1

commit v5 on v4

--- a/solution.py
+++ b/solution.py
@@ -121,25 +121,69 @@
     return lax.axis_index("rows"), lax.axis_index("cols")
 
 
-def greet(rows):
+def div(a, n):
+    return a // n if isinstance(a, int) else lax.div(a, jnp.int32(n))
+
+
+def rem(a, n):
+    return a % n if isinstance(a, int) else lax.rem(a, jnp.int32(n))
+
+
+def place():
     r, c = here()
+    return rem(c, 4), div(r, 16) * 2 + div(c, 4), rem(div(r, 2), 8), rem(r, 2)
+
+
+def at_place(x, y, z, core):
+    return div(y, 2) * 16 + z * 2 + core, rem(y, 2) * 4 + x
+
+
+DY_ORDER = (1, 7, 2, 6, 3, 5, 4, 0)
+OFFSETS = tuple(
+    (dy, (q + k) % 8, core)
+    for core in range(2)
+    for q in range(8)
+    for k, dy in enumerate(DY_ORDER)
+    if (dy, (q + k) % 8, core) != (0, 0, 0)
+)
+
+
+def signal(peer):
     barrier = pltpu.get_barrier_semaphore()
+    pl.semaphore_signal(barrier, inc=1, device_id=peer, device_id_type=MESH)
+
+
+def greet_cols():
+    r, c = here()
     for i in range(1, COLS):
-        peer = (r, lax.rem(c + i, COLS))
-        pl.semaphore_signal(barrier, inc=1, device_id=peer, device_id_type=MESH)
-    if rows:
-
-        def signal(i, _):
-            peer = (lax.rem(r + i, ROWS), c)
-            pl.semaphore_signal(barrier, inc=1, device_id=peer, device_id_type=MESH)
-            return 0
-
-        lax.fori_loop(1, ROWS, signal, 0)
-
-
-def gather(rows):
-    count = COLS - 1 + (ROWS - 1 if rows else 0)
+        signal((r, lax.rem(c + i, COLS)))
+
+
+def greet_plane(part):
+    x, y, z, core = place()
+    if part == 0:
+        for i in range(1, 4):
+            signal(at_place(rem(x + i, 4), y, z, core))
+    for dy, dz, dc in OFFSETS[part::8]:
+        signal(at_place(x, rem(y + dy, 8), rem(z + dz, 8), rem(core + dc, 2)))
+
+
+def gather(count):
     pl.semaphore_wait(pltpu.get_barrier_semaphore(), count)
+
+
+PLANE = 3 + len(OFFSETS)
+
+
+def remote(src, dst, sems, peer):
+    pltpu.make_async_remote_copy(
+        src_ref=src,
+        dst_ref=dst,
+        send_sem=sems[0],
+        recv_sem=sems[1],
+        device_id=peer,
+        device_id_type=MESH,
+    ).start()
 
 
 def to_col(peer, src, dst, sems):
@@ -147,14 +191,20 @@
 
     @pl.when(peer != c)
     def _():
-        pltpu.make_async_remote_copy(
-            src_ref=src.at[peer],
-            dst_ref=dst.at[c],
-            send_sem=sems[0],
-            recv_sem=sems[1],
-            device_id=(r, peer),
-            device_id_type=MESH,
-        ).start()
+        remote(src.at[peer], dst.at[c], sems, (r, peer))
+
+
+def to_x(peer, src, dst, send, near, far):
+    x, y, z, core = place()
+    partner = x + 1 - 2 * rem(x, 2)
+
+    @pl.when(peer == partner)
+    def _():
+        remote(src.at[peer], dst.at[x], (send, near), at_place(peer, y, z, core))
+
+    @pl.when(div(peer, 2) != div(x, 2))
+    def _():
+        remote(src.at[peer], dst.at[x], (send, far), at_place(peer, y, z, core))
 
 
 def finish(ref, count, sem):
@@ -162,24 +212,46 @@
     pltpu.make_async_copy(part, part, sem).wait()
 
 
-def to_rows(src, dst, sems):
+def exchange_plane(s1, r1, o, sems):
+    x, y, z, core = place()
     r, c = here()
-
-    def send(i, _):
-        peer = lax.rem(r + i, ROWS)
-        pltpu.make_async_remote_copy(
-            src_ref=src.at[:, peer],
-            dst_ref=dst.at[r],
-            send_sem=sems[0],
-            recv_sem=sems[1],
-            device_id=(peer, c),
-            device_id_type=MESH,
-        ).start()
-        return 0
-
-    lax.fori_loop(1, ROWS, send, 0)
-    dst[r] = src[:, r]
-    finish(dst, ROWS - 1, sems[1])
+    send1, near, far, send2, recv2 = sems
+    r1[x] = s1[x]
+    for step in range(2):
+        finish(r1, 1 + step, (near, far)[step])
+        first = 2 * rem(div(x, 2) + step, 2)
+        planes = [rem(y + dy, 8) for dy in DY_ORDER]
+        bases = [(div(yy, 2) * 16, rem(yy, 2)) for yy in planes]
+        mine = o.at[r, pl.ds(rem(y, 2) * 4 + first, 2)]
+
+        def row(q, _):
+            dc = div(q, 8)
+            side = rem(core + dc, 2)
+            for k, dy in enumerate(DY_ORDER):
+                dz = rem(q + k, 8)
+                line = bases[k][0] + rem(z + dz, 8) * 2 + side
+                half = bases[k][1]
+
+                def go():
+                    remote(
+                        r1.at[pl.ds(first, 2), half * 64 + line],
+                        mine,
+                        (send2, recv2),
+                        (line, half * 4 + x),
+                    )
+
+                if dy == 0:
+                    pl.when(dz + dc > 0)(go)
+                else:
+                    go()
+            return 0
+
+        lax.fori_loop(0, 16, row, 0)
+    o[r, pl.ds(rem(y, 2) * 4, 4)] = r1[:, rem(y, 2) * 64 + r]
+    finish(s1, 3, send1)
+    part = s1.at[:, pl.ds(0, 127)]
+    pltpu.make_async_copy(part, part, recv2).wait()
+    pltpu.make_async_copy(part, part, send2).wait()
 
 
 def spread(x, join):
@@ -217,7 +289,7 @@
 def pull_kernel(net, x, before, after, slopes, tile, rshift, pshift, frac, o, s1, padded, spots, wts, sc, *sems):
     own = here()[1] if net else 0
     if net:
-        greet(False)
+        greet_cols()
     padded[:, 0:HALO, :] = before[...].astype(F32)
     padded[:, HALO : HALO + 128, :] = x[...].astype(F32)
     padded[:, HALO + 128 :, :] = after[...].astype(F32)
@@ -289,7 +361,7 @@
 
             @pl.when(n == 1)
             def _():
-                gather(False)
+                gather(COLS - 1)
 
             @pl.when(n > 0)
             def _():
@@ -307,11 +379,11 @@
 
 
 def column_kernel(net, g, d1, tw, f2, m0, o, s1, r1, ure, uim, *sems):
-    if net:
-        greet(True)
     flat = s1.reshape(1024, 128) if net else s1
     cos, sin = tw[0], tw[1]
     for grp in range(8):
+        if net:
+            greet_plane(grp)
         x, at = [], []
         for i in (2 * grp, 2 * grp + 1):
             x += decode(g[pl.ds(i, 64, stride=16), :])
@@ -327,9 +399,8 @@
     def send(kg):
         if net and kg >= 0:
             if kg == 0:
-                gather(True)
-            to_col(kg, s1, r1, sems[:2])
-            to_col(kg + 4, s1, r1, sems[:2])
+                gather(PLANE)
+            to_x(kg, s1, r1, *sems[:3])
 
     for kg in range(4):
         rows = slice(kg * 256, (kg + 1) * 256)
@@ -342,26 +413,21 @@
                 part = jnp.where(lane < 32, special, part)
             word = encode(part[:128], part[128:])
             for half in range(2):
-                at = pl.ds((half * 4 + kg) * 128 + h, 64, stride=2)
+                at = pl.ds((kg * 2 + half) * 128 + h, 64, stride=2)
                 flat[at, :] = word[half * 64 : half * 64 + 64]
         send(kg - 1)
     send(3)
     if net:
-        own = here()[1]
-        r1[own] = s1[own]
-        finish(r1, COLS - 1, sems[1])
-        to_rows(r1, o, sems[2:])
-        finish(s1, COLS - 1, sems[0])
-        finish(o, ROWS - 1, sems[2])
+        exchange_plane(s1, r1, o, sems)
     else:
         o[...] = s1[...]
 
 
 def row_kernel(net, kb, x, e, tw, w2, ka_ref, w3, e4, o, s1, r1, uh, ul, sh, sl, yh, yl, *sems):
-    if net:
-        greet(True)
     flat = s1.reshape(512, 128) if net else s1
     for c in range(8):
+        if net:
+            greet_plane(c)
         cos = jnp.concatenate([tw[0, c * 16 : c * 16 + 16, :]] * 8, 0)
         sin = jnp.concatenate([tw[1, c * 16 : c * 16 + 16, :]] * 8, 0)
         for h in range(2):
@@ -409,29 +475,27 @@
                 at = pl.ds(c * 128 + col * 16, 16)
                 yh[at, :] = y[0][c * 16 : c * 16 + 16]
                 yl[at, :] = y[1][c * 16 : c * 16 + 16]
-    for c in range(8):
-        rows = slice(c * 128, (c + 1) * 128)
-        out = dot3(pair(e4), (yh[rows, :], yl[rows, :]), True)
-        flat[c * 64 : c * 64 + 64, :] = encode(out[:64], out[64:])
-        if net and c == 1:
-            gather(True)
-        if net and c > 0:
-            to_col(c - 1, s1, r1, sems[:2])
+    for peer in range(4):
+        for half in range(2):
+            c = half * 4 + peer
+            rows = slice(c * 128, (c + 1) * 128)
+            out = dot3(pair(e4), (yh[rows, :], yl[rows, :]), True)
+            at = (peer * 2 + half) * 64
+            flat[at : at + 64, :] = encode(out[:64], out[64:])
+        if net and peer == 1:
+            gather(PLANE)
+        if net and peer > 0:
+            to_x(peer - 1, s1, r1, *sems[:3])
     if net:
-        to_col(COLS - 1, s1, r1, sems[:2])
-        own = here()[1]
-        r1[own] = s1[own]
-        finish(r1, COLS - 1, sems[1])
-        to_rows(r1, o, sems[2:])
-        finish(s1, COLS - 1, sems[0])
-        finish(o, ROWS - 1, sems[2])
+        to_x(3, s1, r1, *sems[:3])
+        exchange_plane(s1, r1, o, sems)
     else:
         o[...] = s1[...]
 
 
 def image_kernel(net, t, f4, m0i, tw, d4, o, s1, r1, vre, vim, *sems):
     if net:
-        greet(False)
+        greet_cols()
     flat = s1.reshape(512, 128) if net else s1
     for kg in range(4):
         block = decode(t[pl.ds(kg, 128, stride=4), :])
@@ -459,7 +523,7 @@
             word = encode(out[:, j * 256 : j * 256 + 128], out[:, j * 256 + 128 : j * 256 + 256])
             flat[pl.ds(grp * 2 + j, 64, stride=8), :] = word
     if net:
-        gather(False)
+        gather(COLS - 1)
         own = here()[1]
         for i in range(1, COLS):
             to_col(lax.rem(own + i, COLS), s1, r1, sems)
@@ -477,14 +541,14 @@
         finish(s1, COLS - 1, sems[0])
 
 
-def call(kernel, out, scratch, *args, net=None, phases=1, smem=()):
+def call(kernel, out, scratch, *args, net=None, phases=2, smem=()):
     specs = [
         pl.BlockSpec(memory_space=pltpu.SMEM if i in smem else pltpu.VMEM)
         for i in range(len(args))
     ]
     params = {}
     if net is not None:
-        scratch = scratch + [pltpu.SemaphoreType.DMA] * (2 * phases)
+        scratch = scratch + [pltpu.SemaphoreType.DMA] * phases
         params["compiler_params"] = pltpu.CompilerParams(collective_id=net, has_side_effects=True)
     return pl.pallas_call(
         functools.partial(kernel, net is not None),
@@ -526,9 +590,9 @@
     return call(
         column_kernel,
         ((64, 8, 2, 128) if net is not None else (1024, 128), jnp.int32),
-        [words(8, 64, 2, 128) if net is not None else words(1024, 128)] * 2 + [pltpu.VMEM((1024, 128), F32)] * 2,
+        [words(4, 128, 2, 128) if net is not None else words(1024, 128)] * 2 + [pltpu.VMEM((1024, 128), F32)] * 2,
         g, two(t["d1"]), jnp.asarray(t["tw1"]), two(t["f2"]), two(t["m0"]),
-        net=net, phases=2,
+        net=net, phases=5,
     )
 
 
@@ -541,12 +605,12 @@
     return call(
         row_kernel,
         ((64, 8, 1, 128) if net is not None else (512, 128), jnp.int32),
-        [words(8, 64, 1, 128) if net is not None else words(512, 128)] * 2
+        [words(4, 128, 1, 128) if net is not None else words(512, 128)] * 2
         + [pltpu.VMEM((2048, 128), BF16)] * 4
         + [pltpu.VMEM((1024, 128), BF16)] * 2,
         kb, x, two(t["e"]), jnp.asarray(t["tw2"]), two(t["w2"]), jnp.asarray(t["ka"]),
         two(t["w3"]), two(t["e4"]),
-        smem=(0,), net=net, phases=2,
+        smem=(0,), net=net, phases=5,
     )
 
 

time: 109 us -> 114 us (1.046)
  Pallas kernels: 93.2 us -> 98.8 us
    pallas_call x4, Pallas kernels: 93.2 us -> 98.8 us  [call(): pl.pallas_call(functools.partial(kernel, net is not None), out_shape=jax....]
where the time goes in v5:
time: 114 us
  Pallas kernels  98.8 us (87%)
  starting transfers between devices  10.7 us (9%)
  local copies, waits for them, and re-layouts  3.28 us (3%)
    pallas_call x4, Pallas kernels, call(): pl.pallas_call(functools.partial(kernel, net is not None), out_shape=jax....  98.8 us
    ppermute x1, starting transfers between devices, per_device(): after = lax.ppermute(residual[:, :HALO], 'rows', down)  8.73 us
    unnamed x5, local copies, waits for them, and re-layouts  2.5 us
  transfers between devices with their start and end apart: 2, of which 1 were waited for; matrix products, arithmetic and copies ran while one was open for 1% of the time, Pallas kernels for 0%

profile of v5, /device:TPU:1, one launch (start us, length us, event | category | flops | bytes accessed | tf_op | source)
XLA Modules:
  0.0 114.0 jit_solution(17752384367489926058)
XLA Ops:
  0.0 0.8 fusion.3
  0.8 8.7 %collective-permute-start.1 = (bf16[2,8,1024]{2,1,0:T(8,128)(2,1)S(1)}, bf16[2,8,1024]{2,1,0:T(8,128)(2,1)S(1)}, u32[]{:S(2)}, u32[]{:S(2)}) collective-permute-start(bf16[2,8,1024]{2,1,0:T(8,128)(2,1)S(1)} %get-tuple-element.5), channel_id=1, source_target_pairs={{8,0},{16,8},{24,16},{32,24},{40,32},{48,40},{56,48},{64,56},{72,6... | collective-permute-start | bytes 98312 | tf_op jit(solution)/shard_map/ppermute | solution.py:633
  9.5 1.9 %collective-permute-start = (bf16[2,8,1024]{2,1,0:T(8,128)(2,1)S(1)}, bf16[2,8,1024]{2,1,0:T(8,128)(2,1)S(1)}, u32[]{:S(2)}, u32[]{:S(2)}) collective-permute-start(bf16[2,8,1024]{2,1,0:T(8,128)(2,1)S(1)} %get-tuple-element.6), channel_id=1, source_target_pairs={{0,8},{8,16},{16,24},{24,32},{32,40},{40,48},{48,56},{56,64},{64,7... | collective-permute-start | bytes 98312 | tf_op jit(solution)/shard_map/ppermute | solution.py:632
  11.5 0.6 fusion.2.kb
  12.1 0.0 collective-permute-done.1.after
  12.1 0.0 copy-start
  12.1 0.6 collective-permute-done.before
  12.6 0.0 copy-start.1
  12.6 0.1 copy-done
  12.7 0.6 copy-done.1
  13.2 13.3 %shard_map.181 = s32[8,128,128]{2,1,0:T(8,128)} custom-call(bf16[2,128,1024]{2,1,0:T(8,128)(2,1)} %x.1, bf16[2,8,1024]{2,1,0:T(8,128)(2,1)} %copy-done.1, bf16[2,8,1024]{2,1,0:T(8,128)(2,1)} %copy-done, bf16[4,128,1024]{2,1,0:T(8,128)(2,1)} %slopes.1, s32[2,8,128]{2,1,0:T(8,128)} %bitcast.10, s32[2,8,128]{2,1,0:T(8,128)} %bitcast.11, s32[2,8,128]{2,1,0:T(8,128)} %bitcast.12, ...), custom_call_target="tpu_custom_call" | custom-call | tf_op jit(solution)/shard_map/pallas_call | solution.py:553
  26.6 42.7 %shard_map.182 = s32[64,8,2,128]{3,2,1,0:T(2,128)} custom-call(s32[1024,128]{1,0:T(8,128)} %bitcast.8, bf16[2,64,64]{2,1,0:T(8,128)(2,1)} %constant.76.clone.d1, f32[2,32,128]{2,1,0:T(8,128)} %constant.77.clone.tw, bf16[2,256,256]{2,1,0:T(8,128)(2,1)} %constant.78.clone.f2, bf16[2,256,256]{2,1,0:T(8,128)(2,1)} %constant.79.clone.m0), custom_call_target="tpu_custom_call" | custom-call | tf_op jit(solution)/shard_map/pallas_call | solution.py:553
  69.3 29.4 %shard_map.183 = s32[64,8,1,128]{3,2,1,0:T(1,128)} custom-call(f32[8]{0:T(128)} %fusion.2.kb, s32[1024,128]{1,0:T(8,128)} %bitcast.7, bf16[2,128,256]{2,1,0:T(8,128)(2,1)} %constant.80.clone.e, f32[2,128,128]{2,1,0:T(8,128)} %constant.81.clone.tw, bf16[2,128,256]{2,1,0:T(8,128)(2,1)} %constant.82.clone.w2, f32[128,128]{1,0:T(8,128)} %constant.83.clone.ka_ref, ...), custom_call_target="tpu_custom_call" | custom-call | tf_op jit(solution)/shard_map/pallas_call | solution.py:553
  98.8 13.3 %shard_map.184 = f32[128,1024]{1,0:T(8,128)} custom-call(s32[512,128]{1,0:T(8,128)} %bitcast.9, bf16[2,256,256]{2,1,0:T(8,128)(2,1)} %constant.86.clone.f4, bf16[2,256,256]{2,1,0:T(8,128)(2,1)} %constant.87.clone.m0i, f32[2,32,128]{2,1,0:T(8,128)} %constant.77.clone.tw, bf16[2,64,64]{2,1,0:T(8,128)(2,1)} %constant.88.clone.d4), custom_call_target="tpu_custom_call" | custom-call | tf_op jit(solution)/shard_map/pallas_call | solution.py:553
  112.1 1.9 %copy.21 = f32[128,1024]{1,0:T(8,128)} copy(f32[128,1024]{1,0:T(8,128)} %shard_map.184) | data formatting | bytes 1048576
Async XLA Ops:
  0.8 11.3 %collective-permute-start.1 = (bf16[2,8,1024]{2,1,0:T(8,128)(2,1)S(1)}, bf16[2,8,1024]{2,1,0:T(8,128)(2,1)S(1)}, u32[]{:S(2)}, u32[]{:S(2)}) collective-permute-start(bf16[2,8,1024]{2,1,0:T(8,128)(2,1)S(1)} %get-tuple-element.5), channel_id=1, source_target_pairs={{8,0},{16,8},{24,16},{32,24},{40,32},{48,40},{56,48},{64,56},{72,6... | collective-permute-start | bytes 98312 | tf_op jit(solution)/shard_map/ppermute | solution.py:633
  9.5 3.1 %collective-permute-start = (bf16[2,8,1024]{2,1,0:T(8,128)(2,1)S(1)}, bf16[2,8,1024]{2,1,0:T(8,128)(2,1)S(1)}, u32[]{:S(2)}, u32[]{:S(2)}) collective-permute-start(bf16[2,8,1024]{2,1,0:T(8,128)(2,1)S(1)} %get-tuple-element.6), channel_id=1, source_target_pairs={{0,8},{8,16},{16,24},{24,32},{32,40},{40,48},{48,56},{56,64},{64,7... | collective-permute-start | bytes 98312 | tf_op jit(solution)/shard_map/ppermute | solution.py:632
  12.1 0.6 copy-start
  12.6 0.6 copy-start.1

commit v6 on v4

--- a/solution.py
+++ b/solution.py
@@ -121,40 +121,47 @@
     return lax.axis_index("rows"), lax.axis_index("cols")
 
 
-def greet(rows):
+def greet():
     r, c = here()
     barrier = pltpu.get_barrier_semaphore()
     for i in range(1, COLS):
         peer = (r, lax.rem(c + i, COLS))
         pl.semaphore_signal(barrier, inc=1, device_id=peer, device_id_type=MESH)
-    if rows:
-
-        def signal(i, _):
-            peer = (lax.rem(r + i, ROWS), c)
-            pl.semaphore_signal(barrier, inc=1, device_id=peer, device_id_type=MESH)
-            return 0
-
-        lax.fori_loop(1, ROWS, signal, 0)
-
-
-def gather(rows):
-    count = COLS - 1 + (ROWS - 1 if rows else 0)
-    pl.semaphore_wait(pltpu.get_barrier_semaphore(), count)
-
-
-def to_col(peer, src, dst, sems):
+
+    def signal(i, _):
+        peer = (lax.rem(r + i, ROWS), c)
+        pl.semaphore_signal(barrier, inc=1, device_id=peer, device_id_type=MESH)
+        return 0
+
+    lax.fori_loop(1, ROWS, signal, 0)
+
+
+def gather():
+    pl.semaphore_wait(pltpu.get_barrier_semaphore(), COLS - 1 + ROWS - 1)
+
+
+def remote(src, dst, sems, peer):
+    pltpu.make_async_remote_copy(
+        src_ref=src,
+        dst_ref=dst,
+        send_sem=sems[0],
+        recv_sem=sems[1],
+        device_id=peer,
+        device_id_type=MESH,
+    ).start()
+
+
+def to_col(peer, src, dst, send, near, far):
     r, c = here()
-
-    @pl.when(peer != c)
+    same = lax.div(c, 4) == peer // 4 if isinstance(peer, int) else lax.div(c, 4) == lax.div(peer, 4)
+
+    @pl.when(same & (peer != c))
     def _():
-        pltpu.make_async_remote_copy(
-            src_ref=src.at[peer],
-            dst_ref=dst.at[c],
-            send_sem=sems[0],
-            recv_sem=sems[1],
-            device_id=(r, peer),
-            device_id_type=MESH,
-        ).start()
+        remote(src.at[peer], dst.at[c], (send, near), (r, peer))
+
+    @pl.when(jnp.logical_not(same))
+    def _():
+        remote(src.at[peer], dst.at[c], (send, far), (r, peer))
 
 
 def finish(ref, count, sem):
@@ -162,24 +169,36 @@
     pltpu.make_async_copy(part, part, sem).wait()
 
 
-def to_rows(src, dst, sems):
+def to_rows(src, dst, sems, first, count):
     r, c = here()
 
     def send(i, _):
-        peer = lax.rem(r + i, ROWS)
-        pltpu.make_async_remote_copy(
-            src_ref=src.at[:, peer],
-            dst_ref=dst.at[r],
-            send_sem=sems[0],
-            recv_sem=sems[1],
-            device_id=(peer, c),
-            device_id_type=MESH,
-        ).start()
+        peer = lax.rem(r + lax.rem(i * 27, ROWS), ROWS)
+        remote(
+            src.at[pl.ds(first, count), peer], dst.at[r, pl.ds(first, count)], sems, (peer, c)
+        )
         return 0
 
     lax.fori_loop(1, ROWS, send, 0)
-    dst[r] = src[:, r]
-    finish(dst, ROWS - 1, sems[1])
+
+
+def all_exchange(s1, r1, o, sems, split_groups):
+    send1, near, far, send2, recv2 = sems
+    r, c = here()
+    r1[c] = s1[c]
+    own = lax.div(c, 4) * 4
+    finish(r1, 3, near)
+    if split_groups:
+        to_rows(r1, o, (send2, recv2), own, 4)
+        finish(r1, 4, far)
+        to_rows(r1, o, (send2, recv2), 4 - own, 4)
+    else:
+        finish(r1, 4, far)
+        to_rows(r1, o, (send2, recv2), 0, 8)
+    o[r] = r1[:, r]
+    finish(o, ROWS - 1, recv2)
+    finish(s1, COLS - 1, send1)
+    finish(o, ROWS - 1, send2)
 
 
 def spread(x, join):
@@ -216,8 +235,6 @@
 
 def pull_kernel(net, x, before, after, slopes, tile, rshift, pshift, frac, o, s1, padded, spots, wts, sc, *sems):
     own = here()[1] if net else 0
-    if net:
-        greet(False)
     padded[:, 0:HALO, :] = before[...].astype(F32)
     padded[:, HALO : HALO + 128, :] = x[...].astype(F32)
     padded[:, HALO + 128 :, :] = after[...].astype(F32)
@@ -289,26 +306,25 @@
 
             @pl.when(n == 1)
             def _():
-                gather(False)
+                gather()
 
             @pl.when(n > 0)
             def _():
-                to_col(lax.rem(own + n, COLS), s1, o, sems)
+                to_col(lax.rem(own + n, COLS), s1, o, *sems)
 
         return 0
 
     lax.fori_loop(0, 8, block, 0)
     if net:
         o[own] = s1[own]
-        finish(o, COLS - 1, sems[1])
+        finish(o, 3, sems[1])
+        finish(o, 4, sems[2])
         finish(s1, COLS - 1, sems[0])
     else:
         o[...] = s1[...]
 
 
 def column_kernel(net, g, d1, tw, f2, m0, o, s1, r1, ure, uim, *sems):
-    if net:
-        greet(True)
     flat = s1.reshape(1024, 128) if net else s1
     cos, sin = tw[0], tw[1]
     for grp in range(8):
@@ -326,10 +342,8 @@
 
     def send(kg):
         if net and kg >= 0:
-            if kg == 0:
-                gather(True)
-            to_col(kg, s1, r1, sems[:2])
-            to_col(kg + 4, s1, r1, sems[:2])
+            to_col(kg, s1, r1, *sems[:3])
+            to_col(kg + 4, s1, r1, *sems[:3])
 
     for kg in range(4):
         rows = slice(kg * 256, (kg + 1) * 256)
@@ -347,19 +361,12 @@
         send(kg - 1)
     send(3)
     if net:
-        own = here()[1]
-        r1[own] = s1[own]
-        finish(r1, COLS - 1, sems[1])
-        to_rows(r1, o, sems[2:])
-        finish(s1, COLS - 1, sems[0])
-        finish(o, ROWS - 1, sems[2])
+        all_exchange(s1, r1, o, sems, True)
     else:
         o[...] = s1[...]
 
 
 def row_kernel(net, kb, x, e, tw, w2, ka_ref, w3, e4, o, s1, r1, uh, ul, sh, sl, yh, yl, *sems):
-    if net:
-        greet(True)
     flat = s1.reshape(512, 128) if net else s1
     for c in range(8):
         cos = jnp.concatenate([tw[0, c * 16 : c * 16 + 16, :]] * 8, 0)
@@ -413,25 +420,17 @@
         rows = slice(c * 128, (c + 1) * 128)
         out = dot3(pair(e4), (yh[rows, :], yl[rows, :]), True)
         flat[c * 64 : c * 64 + 64, :] = encode(out[:64], out[64:])
-        if net and c == 1:
-            gather(True)
         if net and c > 0:
-            to_col(c - 1, s1, r1, sems[:2])
+            to_col(c - 1, s1, r1, *sems[:3])
     if net:
-        to_col(COLS - 1, s1, r1, sems[:2])
-        own = here()[1]
-        r1[own] = s1[own]
-        finish(r1, COLS - 1, sems[1])
-        to_rows(r1, o, sems[2:])
-        finish(s1, COLS - 1, sems[0])
-        finish(o, ROWS - 1, sems[2])
+        to_col(COLS - 1, s1, r1, *sems[:3])
+        all_exchange(s1, r1, o, sems, False)
     else:
         o[...] = s1[...]
 
 
 def image_kernel(net, t, f4, m0i, tw, d4, o, s1, r1, vre, vim, *sems):
-    if net:
-        greet(False)
+
     flat = s1.reshape(512, 128) if net else s1
     for kg in range(4):
         block = decode(t[pl.ds(kg, 128, stride=4), :])
@@ -459,12 +458,12 @@
             word = encode(out[:, j * 256 : j * 256 + 128], out[:, j * 256 + 128 : j * 256 + 256])
             flat[pl.ds(grp * 2 + j, 64, stride=8), :] = word
     if net:
-        gather(False)
         own = here()[1]
         for i in range(1, COLS):
-            to_col(lax.rem(own + i, COLS), s1, r1, sems)
+            to_col(lax.rem(own + i, COLS), s1, r1, *sems)
         r1[own] = s1[own]
-        finish(r1, COLS - 1, sems[1])
+        finish(r1, 3, sems[1])
+        finish(r1, 4, sems[2])
     else:
         r1[...] = s1[...]
     for c in range(8):
@@ -475,6 +474,32 @@
                 o[at, ph * 128 : ph * 128 + 128] = halves[it][ph * 8 : ph * 8 + 8]
     if net:
         finish(s1, COLS - 1, sems[0])
+
+
+def whole_kernel(
+    kb, x, before, after, slopes, tile, rshift, pshift, frac,
+    d1, tw1, f2, m0, e, tw2, w2, ka, w3, e4, f4, m0i, d4, out, *rest,
+):
+    scratch, sems = rest[:-16], rest[-16:]
+    flow_land, s_flow, spec_land, s_spec, r_spec, mix_land, s_mix, r_mix, s_img, r_img = scratch[:10]
+    padded, spots, wts, sc, ure, uim, uh, ul, sh, sl, yh, yl, vre, vim = scratch[10:]
+    greet()
+    pull_kernel(
+        True, x, before, after, slopes, tile, rshift, pshift, frac,
+        flow_land, s_flow, padded, spots, wts, sc, *sems[:3],
+    )
+    column_kernel(
+        True, flow_land.reshape(1024, 128), d1, tw1, f2, m0,
+        spec_land, s_spec, r_spec, ure, uim, *sems[3:8],
+    )
+    row_kernel(
+        True, kb, spec_land.reshape(1024, 128), e, tw2, w2, ka, w3, e4,
+        mix_land, s_mix, r_mix, uh, ul, sh, sl, yh, yl, *sems[8:13],
+    )
+    image_kernel(
+        True, mix_land.reshape(512, 128), f4, m0i, tw1, d4,
+        out, s_img, r_img, vre, vim, *sems[13:16],
+    )
 
 
 def call(kernel, out, scratch, *args, net=None, phases=1, smem=()):
@@ -561,20 +586,53 @@
     )
 
 
+def wave_of_columns(device):
+    group, low = device // 4, device % 4
+    kk = low * 8 + jnp.arange(8, dtype=jnp.int32)
+    b = kk + 64 * group + jnp.where((kk == 0) & (group >= 64), 32, 0)
+    return jnp.where(b > N // 2, b - N, b).astype(F32) * (2.0 * math.pi / N)
+
+
 def per_device(residual, field_slopes, source_tile, row_shift, pixel_shift, fraction):
     peers = lax.axis_size("rows")
     up = [(i, i + 1) for i in range(peers - 1)]
     down = [(j, i) for i, j in up]
     before = lax.ppermute(residual[:, -HALO:], "rows", up)
     after = lax.ppermute(residual[:, :HALO], "rows", down)
-    flow = pull(
-        residual, before, after, field_slopes, source_tile, row_shift, pixel_shift, fraction,
-        net=0,
-    )
-    spectra = column_transform(flow.reshape(1024, 128), net=1)
     device = lax.axis_index("rows") * lax.axis_size("cols") + lax.axis_index("cols")
-    mixed = row_transform(spectra.reshape(1024, 128), device, net=2)
-    return image_transform(mixed.reshape(512, 128), net=3)
+    flip = lambda y: jnp.transpose(y, (0, 2, 1))
+    t = tables()
+    plain = lambda name: jnp.asarray(t[name])
+    args = (
+        wave_of_columns(device), residual, before, after, field_slopes,
+        flip(source_tile), flip(row_shift), flip(pixel_shift), flip(fraction),
+        two(t["d1"]), plain("tw1"), two(t["f2"]), two(t["m0"]), two(t["e"]), plain("tw2"),
+        two(t["w2"]), plain("ka"), two(t["w3"]), two(t["e4"]), two(t["f4"]), two(t["m0i"]),
+        two(t["d4"]),
+    )
+    f32 = lambda *shape: pltpu.VMEM(shape, F32)
+    bf16 = lambda *shape: pltpu.VMEM(shape, BF16)
+    scratch = (
+        [words(8, 128, 128)] * 2
+        + [words(64, 8, 2, 128)] + [words(8, 64, 2, 128)] * 2
+        + [words(64, 8, 1, 128)] + [words(8, 64, 1, 128)] * 2
+        + [words(8, 64, 128)] * 2
+        + [f32(2, 144, 1024), words(16, 128), f32(6, 16, 128), f32(2, 2, 144, 128)]
+        + [f32(1024, 128)] * 2
+        + [bf16(2048, 128)] * 4 + [bf16(1024, 128)] * 2
+        + [f32(512, 128)] * 2
+        + [pltpu.SemaphoreType.DMA] * 16
+    )
+    return pl.pallas_call(
+        whole_kernel,
+        out_shape=jax.ShapeDtypeStruct((128, 1024), F32),
+        in_specs=[
+            pl.BlockSpec(memory_space=pltpu.VMEM if i else pltpu.SMEM) for i in range(len(args))
+        ],
+        out_specs=pl.BlockSpec(memory_space=pltpu.VMEM),
+        scratch_shapes=scratch,
+        compiler_params=pltpu.CompilerParams(collective_id=0, has_side_effects=True),
+    )(*args)
 
 
 def solution(mesh):

time: 109 us -> 98.7 us (0.906)
  Pallas kernels: 93.2 us -> 83.3 us
    pallas_call x4 -> x1, Pallas kernels: 93.2 us -> 83.3 us  [per_device(): pl.pallas_call(whole_kernel, out_shape=jax.ShapeDtypeStruct((128, 1024),...]
where the time goes in v6:
time: 98.7 us; the launch traced here: 98.5 us
  Pallas kernels  83.3 us (84%)
  starting transfers between devices  10.7 us (11%)
  local copies, waits for them, and re-layouts  3.28 us (3%)
    pallas_call x1, Pallas kernels, per_device(): pl.pallas_call(whole_kernel, out_shape=jax.ShapeDtypeStruct((128, 1024),...  83.3 us
    ppermute x1, starting transfers between devices, per_device(): after = lax.ppermute(residual[:, :HALO], 'rows', down)  8.73 us
    unnamed x5, local copies, waits for them, and re-layouts  2.5 us
  transfers between devices with their start and end apart: 2, of which 1 were waited for; matrix products, arithmetic and copies ran while one was open for 1% of the time, Pallas kernels for 0%

profile of v6, /device:TPU:1, one launch (start us, length us, event | category | flops | bytes accessed | tf_op | source)
XLA Modules:
  0.0 98.5 jit_solution(7937660376511022346)
XLA Ops:
  0.0 0.8 fusion.3
  0.8 8.7 %collective-permute-start.1 = (bf16[2,8,1024]{2,1,0:T(8,128)(2,1)S(1)}, bf16[2,8,1024]{2,1,0:T(8,128)(2,1)S(1)}, u32[]{:S(2)}, u32[]{:S(2)}) collective-permute-start(bf16[2,8,1024]{2,1,0:T(8,128)(2,1)S(1)} %get-tuple-element.5), channel_id=1, source_target_pairs={{8,0},{16,8},{24,16},{32,24},{40,32},{48,40},{56,48},{64,56},{72,6... | collective-permute-start | bytes 98312 | tf_op jit(solution)/shard_map/ppermute | solution.py:601
  9.5 1.9 %collective-permute-start = (bf16[2,8,1024]{2,1,0:T(8,128)(2,1)S(1)}, bf16[2,8,1024]{2,1,0:T(8,128)(2,1)S(1)}, u32[]{:S(2)}, u32[]{:S(2)}) collective-permute-start(bf16[2,8,1024]{2,1,0:T(8,128)(2,1)S(1)} %get-tuple-element.6), channel_id=1, source_target_pairs={{0,8},{8,16},{16,24},{24,32},{32,40},{40,48},{48,56},{56,64},{64,7... | collective-permute-start | bytes 98312 | tf_op jit(solution)/shard_map/ppermute | solution.py:600
  11.5 0.5 fusion.2.kb
  12.0 0.0 collective-permute-done.1.after
  12.0 0.0 copy-start
  12.0 0.6 collective-permute-done.before
  12.6 0.0 copy-start.1
  12.6 0.0 copy-done
  12.6 0.6 copy-done.1
  13.2 83.3 %shard_map.181 = f32[128,1024]{1,0:T(8,128)} custom-call(f32[8]{0:T(128)} %fusion.2.kb, bf16[2,128,1024]{2,1,0:T(8,128)(2,1)} %x.1, bf16[2,8,1024]{2,1,0:T(8,128)(2,1)} %copy-done.1, bf16[2,8,1024]{2,1,0:T(8,128)(2,1)} %copy-done, bf16[4,128,1024]{2,1,0:T(8,128)(2,1)} %slopes.1, s32[2,8,128]{2,1,0:T(8,128)} %bitcast.4, s32[2,8,128]{2,1,0:T(8,128)} %bitcast.5, ...), custom_call_target="tpu_custom_call" | custom-call | tf_op jit(solution)/shard_map/pallas_call | solution.py:626
  96.6 1.9 %copy.21 = f32[128,1024]{1,0:T(8,128)} copy(f32[128,1024]{1,0:T(8,128)} %shard_map.181) | data formatting | bytes 1048576
Async XLA Ops:
  0.8 11.2 %collective-permute-start.1 = (bf16[2,8,1024]{2,1,0:T(8,128)(2,1)S(1)}, bf16[2,8,1024]{2,1,0:T(8,128)(2,1)S(1)}, u32[]{:S(2)}, u32[]{:S(2)}) collective-permute-start(bf16[2,8,1024]{2,1,0:T(8,128)(2,1)S(1)} %get-tuple-element.5), channel_id=1, source_target_pairs={{8,0},{16,8},{24,16},{32,24},{40,32},{48,40},{56,48},{64,56},{72,6... | collective-permute-start | bytes 98312 | tf_op jit(solution)/shard_map/ppermute | solution.py:601
  9.5 3.1 %collective-permute-start = (bf16[2,8,1024]{2,1,0:T(8,128)(2,1)S(1)}, bf16[2,8,1024]{2,1,0:T(8,128)(2,1)S(1)}, u32[]{:S(2)}, u32[]{:S(2)}) collective-permute-start(bf16[2,8,1024]{2,1,0:T(8,128)(2,1)S(1)} %get-tuple-element.6), channel_id=1, source_target_pairs={{0,8},{8,16},{16,24},{24,32},{32,40},{40,48},{48,56},{56,64},{64,7... | collective-permute-start | bytes 98312 | tf_op jit(solution)/shard_map/ppermute | solution.py:600
  12.0 0.6 copy-start
  12.6 0.6 copy-start.1

commit v7 on v6

--- a/solution.py
+++ b/solution.py
@@ -233,11 +233,16 @@
     return x * scale, y * scale
 
 
-def pull_kernel(net, x, before, after, slopes, tile, rshift, pshift, frac, o, s1, padded, spots, wts, sc, *sems):
+def pull_kernel(
+    net, x, before, after, slopes, tile, rshift, pshift, frac, o, s1, padded, spots, wts, sc,
+    *link,
+):
     own = here()[1] if net else 0
-    padded[:, 0:HALO, :] = before[...].astype(F32)
+    if net:
+        stage, land, *sems = link
+        stage[0] = x[:, 128 - HALO :, :]
+        stage[1] = x[:, :HALO, :]
     padded[:, HALO : HALO + 128, :] = x[...].astype(F32)
-    padded[:, HALO + 128 :, :] = after[...].astype(F32)
     sc[:, :, 0:8, :] = jnp.zeros((2, 2, 8, 128), F32)
     sc[:, :, 136:144, :] = jnp.zeros((2, 2, 8, 128), F32)
     lane = lax.broadcasted_iota(jnp.int32, (8, 128), 1)
@@ -263,8 +268,7 @@
             )
     place = lax.broadcasted_iota(jnp.int32, (256, 128), 0)
 
-    def block(n, _):
-        b = lax.rem(own + 1 + n, COLS)
+    def block(b):
         r0 = pl.multiple_of(b * 16, 16)
         window = [
             jnp.concatenate(
@@ -302,24 +306,44 @@
             across = -(first * s[0] + second * s[1])
             down = -(first * s[2] + second * s[3])
             s1[b, t * 16 : t * 16 + 16, :] = encode(across, down)
-        if net:
-
-            @pl.when(n == 1)
+
+    def inner(n, _):
+        block(1 + lax.rem(own + n, 6))
+        return 0
+
+    def edge(n, _):
+        block(7 * lax.rem(own + n, 2))
+        return 0
+
+    lax.fori_loop(0, 6, inner, 0)
+    if net:
+        r, c = here()
+        gather()
+        remote(stage.at[0], land.at[0], (sems[3], sems[4]), (lax.rem(r + 1, ROWS), c))
+        remote(stage.at[1], land.at[1], (sems[3], sems[5]), (lax.rem(r + ROWS - 1, ROWS), c))
+        for i in range(1, COLS):
+            peer = lax.rem(own + i, COLS)
+
+            @pl.when((peer > 0) & (peer < COLS - 1))
             def _():
-                gather()
-
-            @pl.when(n > 0)
-            def _():
-                to_col(lax.rem(own + n, COLS), s1, o, *sems)
-
-        return 0
-
-    lax.fori_loop(0, 8, block, 0)
+                to_col(peer, s1, o, *sems[:3])
+
+        finish(land, 1, sems[4])
+        finish(land, 1, sems[5])
+        padded[:, 0:HALO, :] = jnp.where(r > 0, land[0].astype(F32), 0.0)
+        padded[:, HALO + 128 :, :] = jnp.where(r < ROWS - 1, land[1].astype(F32), 0.0)
+    else:
+        padded[:, 0:HALO, :] = before[...].astype(F32)
+        padded[:, HALO + 128 :, :] = after[...].astype(F32)
+    lax.fori_loop(0, 2, edge, 0)
     if net:
         o[own] = s1[own]
+        to_col(0, s1, o, *sems[:3])
+        to_col(COLS - 1, s1, o, *sems[:3])
         finish(o, 3, sems[1])
         finish(o, 4, sems[2])
         finish(s1, COLS - 1, sems[0])
+        finish(stage, 2, sems[3])
     else:
         o[...] = s1[...]
 
@@ -364,6 +388,15 @@
         all_exchange(s1, r1, o, sems, True)
     else:
         o[...] = s1[...]
+
+
+def column_wave(col):
+    r, c = here()
+    group = r * 2 + lax.div(c, 4)
+    b = lax.rem(c, 4) * 8 + col + 64 * group
+    if col == 0:
+        b = b + jnp.where((lax.rem(c, 4) == 0) & (group >= 64), 32, 0)
+    return jnp.where(b > N // 2, b - N, b).astype(F32) * (2.0 * math.pi / N)
 
 
 def row_kernel(net, kb, x, e, tw, w2, ka_ref, w3, e4, o, s1, r1, uh, ul, sh, sl, yh, yl, *sems):
@@ -400,7 +433,7 @@
         for j in range(2):
             col = pr * 2 + j
             out = dot3(pair(w2), (stack(uh, sh, col), stack(ul, sl, col)))
-            wb = kb[col]
+            wb = column_wave(col) if net else kb[col]
             weight = LOCAL_WEIGHT + 1.0 / (ka2 + wb * wb)
             mixed = weight * (wb * out[:, :128] + ka * out[:, 128:])
             q.append(mixed)
@@ -477,23 +510,23 @@
 
 
 def whole_kernel(
-    kb, x, before, after, slopes, tile, rshift, pshift, frac,
+    x, slopes, tile, rshift, pshift, frac,
     d1, tw1, f2, m0, e, tw2, w2, ka, w3, e4, f4, m0i, d4, out, *rest,
 ):
-    scratch, sems = rest[:-16], rest[-16:]
+    scratch, sems = rest[:-19], rest[-19:]
     flow_land, s_flow, spec_land, s_spec, r_spec, mix_land, s_mix, r_mix, s_img, r_img = scratch[:10]
-    padded, spots, wts, sc, ure, uim, uh, ul, sh, sl, yh, yl, vre, vim = scratch[10:]
+    padded, spots, wts, sc, ure, uim, uh, ul, sh, sl, yh, yl, vre, vim, stage, land = scratch[10:]
     greet()
     pull_kernel(
-        True, x, before, after, slopes, tile, rshift, pshift, frac,
-        flow_land, s_flow, padded, spots, wts, sc, *sems[:3],
+        True, x, None, None, slopes, tile, rshift, pshift, frac,
+        flow_land, s_flow, padded, spots, wts, sc, stage, land, *sems[:3], *sems[16:],
     )
     column_kernel(
         True, flow_land.reshape(1024, 128), d1, tw1, f2, m0,
         spec_land, s_spec, r_spec, ure, uim, *sems[3:8],
     )
     row_kernel(
-        True, kb, spec_land.reshape(1024, 128), e, tw2, w2, ka, w3, e4,
+        True, None, spec_land.reshape(1024, 128), e, tw2, w2, ka, w3, e4,
         mix_land, s_mix, r_mix, uh, ul, sh, sl, yh, yl, *sems[8:13],
     )
     image_kernel(
@@ -586,25 +619,12 @@
     )
 
 
-def wave_of_columns(device):
-    group, low = device // 4, device % 4
-    kk = low * 8 + jnp.arange(8, dtype=jnp.int32)
-    b = kk + 64 * group + jnp.where((kk == 0) & (group >= 64), 32, 0)
-    return jnp.where(b > N // 2, b - N, b).astype(F32) * (2.0 * math.pi / N)
-
-
 def per_device(residual, field_slopes, source_tile, row_shift, pixel_shift, fraction):
-    peers = lax.axis_size("rows")
-    up = [(i, i + 1) for i in range(peers - 1)]
-    down = [(j, i) for i, j in up]
-    before = lax.ppermute(residual[:, -HALO:], "rows", up)
-    after = lax.ppermute(residual[:, :HALO], "rows", down)
-    device = lax.axis_index("rows") * lax.axis_size("cols") + lax.axis_index("cols")
     flip = lambda y: jnp.transpose(y, (0, 2, 1))
     t = tables()
     plain = lambda name: jnp.asarray(t[name])
     args = (
-        wave_of_columns(device), residual, before, after, field_slopes,
+        residual, field_slopes,
         flip(source_tile), flip(row_shift), flip(pixel_shift), flip(fraction),
         two(t["d1"]), plain("tw1"), two(t["f2"]), two(t["m0"]), two(t["e"]), plain("tw2"),
         two(t["w2"]), plain("ka"), two(t["w3"]), two(t["e4"]), two(t["f4"]), two(t["m0i"]),
@@ -621,14 +641,13 @@
         + [f32(1024, 128)] * 2
         + [bf16(2048, 128)] * 4 + [bf16(1024, 128)] * 2
         + [f32(512, 128)] * 2
-        + [pltpu.SemaphoreType.DMA] * 16
+        + [bf16(2, 2, 8, 1024)] * 2
+        + [pltpu.SemaphoreType.DMA] * 19
     )
     return pl.pallas_call(
         whole_kernel,
-        out_shape=jax.ShapeDtypeStruct((128, 1024), F32),
-        in_specs=[
-            pl.BlockSpec(memory_space=pltpu.VMEM if i else pltpu.SMEM) for i in range(len(args))
-        ],
+        out_shape=pltpu.VMEM((128, 1024), F32),
+        in_specs=[pl.BlockSpec(memory_space=pltpu.VMEM)] * len(args),
         out_specs=pl.BlockSpec(memory_space=pltpu.VMEM),
         scratch_shapes=scratch,
         compiler_params=pltpu.CompilerParams(collective_id=0, has_side_effects=True),

time: 98.7 us -> 83.9 us (0.85)
  starting transfers between devices: 10.7 us -> 0 us
  local copies, waits for them, and re-layouts: 3.28 us -> 0.8 us
    ppermute x2 -> x0, starting transfers between devices: 10.7 us -> none  [the longest x1 8.73 us: per_device(): after = lax.ppermute(residual[:, :HALO], 'rows', down)]
    unnamed x5 -> x1, local copies, waits for them, and re-layouts: 2.5 us -> 0.8 us
  transfers between devices with their start and end apart: 2 -> 0, of which waited for: 1 -> 0; matrix products, arithmetic and copies ran while one was open for 1% -> 0% of each run, Pallas kernels for 0% -> 0%
where the time goes in v7:
time: 83.9 us; the launch traced here: 83.7 us
  Pallas kernels  82.9 us (99%)
    pallas_call x1, Pallas kernels, per_device(): pl.pallas_call(whole_kernel, out_shape=pltpu.VMEM((128, 1024), F32), in_s...  82.9 us

profile of v7, /device:TPU:1, one launch (start us, length us, event | category | flops | bytes accessed | tf_op | source)
XLA Modules:
  0.0 83.7 jit_solution(2159416219112572891)
XLA Ops:
  0.0 82.9 %shard_map.181 = f32[128,1024]{1,0:T(8,128)S(1)} custom-call(bf16[2,128,1024]{2,1,0:T(8,128)(2,1)} %x.1, bf16[4,128,1024]{2,1,0:T(8,128)(2,1)} %slopes.1, s32[2,8,128]{2,1,0:T(8,128)} %bitcast.4, s32[2,8,128]{2,1,0:T(8,128)} %bitcast.5, s32[2,8,128]{2,1,0:T(8,128)} %bitcast.6, f32[2,8,128]{2,1,0:T(8,128)} %bitcast.7, bf16[2,64,64]{2,1,0:T(8,128)(2,1)} %constant.26.clone.d1, ...), custom_call_target="tpu_custom_call" | custom-call | tf_op jit(solution)/shard_map/pallas_call | solution.py:647
  82.9 0.8 copy.21

commit v8 on v7

--- a/solution.py
+++ b/solution.py
@@ -509,18 +509,29 @@
         finish(s1, COLS - 1, sems[0])
 
 
-def whole_kernel(
-    x, slopes, tile, rshift, pshift, frac,
-    d1, tw1, f2, m0, e, tw2, w2, ka, w3, e4, f4, m0i, d4, out, *rest,
-):
-    scratch, sems = rest[:-19], rest[-19:]
+INPUTS = 19
+
+
+def whole_kernel(*refs):
+    inputs, out, rest = refs[:INPUTS], refs[INPUTS], refs[INPUTS + 1 :]
+    held, scratch, sems = rest[:INPUTS], rest[INPUTS:-20], rest[-20:-1]
     flow_land, s_flow, spec_land, s_spec, r_spec, mix_land, s_mix, r_mix, s_img, r_img = scratch[:10]
     padded, spots, wts, sc, ure, uim, uh, ul, sh, sl, yh, yl, vre, vim, stage, land = scratch[10:]
+    x, slopes, tile, rshift, pshift, frac, d1, tw1, f2, m0, e, tw2, w2, ka, w3, e4, f4, m0i, d4 = held
     greet()
+    loads = [
+        pltpu.make_async_copy(inputs[i], held[i], rest[-1].at[i]) for i in range(INPUTS)
+    ]
+    for load in loads:
+        load.start()
+    for load in loads[:6]:
+        load.wait()
     pull_kernel(
         True, x, None, None, slopes, tile, rshift, pshift, frac,
         flow_land, s_flow, padded, spots, wts, sc, stage, land, *sems[:3], *sems[16:],
     )
+    for load in loads[6:]:
+        load.wait()
     column_kernel(
         True, flow_land.reshape(1024, 128), d1, tw1, f2, m0,
         spec_land, s_spec, r_spec, ure, uim, *sems[3:8],
@@ -633,7 +644,8 @@
     f32 = lambda *shape: pltpu.VMEM(shape, F32)
     bf16 = lambda *shape: pltpu.VMEM(shape, BF16)
     scratch = (
-        [words(8, 128, 128)] * 2
+        [pltpu.VMEM(a.shape, a.dtype) for a in args]
+        + [words(8, 128, 128)] * 2
         + [words(64, 8, 2, 128)] + [words(8, 64, 2, 128)] * 2
         + [words(64, 8, 1, 128)] + [words(8, 64, 1, 128)] * 2
         + [words(8, 64, 128)] * 2
@@ -643,11 +655,12 @@
         + [f32(512, 128)] * 2
         + [bf16(2, 2, 8, 1024)] * 2
         + [pltpu.SemaphoreType.DMA] * 19
+        + [pltpu.SemaphoreType.DMA((INPUTS,))]
     )
     return pl.pallas_call(
         whole_kernel,
         out_shape=pltpu.VMEM((128, 1024), F32),
-        in_specs=[pl.BlockSpec(memory_space=pltpu.VMEM)] * len(args),
+        in_specs=[pl.BlockSpec(memory_space=pl.ANY)] * len(args),
         out_specs=pl.BlockSpec(memory_space=pltpu.VMEM),
         scratch_shapes=scratch,
         compiler_params=pltpu.CompilerParams(collective_id=0, has_side_effects=True),

time: 83.9 us -> 82.1 us (0.979)
  Pallas kernels: 82.9 us -> 81.2 us
    pallas_call x1, Pallas kernels: 82.9 us -> 81.2 us  [per_device(): pl.pallas_call(whole_kernel, out_shape=pltpu.VMEM((128, 1024), F32), in_s...]
where the time goes in v8:
time: 82.1 us; the launch traced here: 82 us
  Pallas kernels  81.2 us (99%)
    pallas_call x1, Pallas kernels, per_device(): pl.pallas_call(whole_kernel, out_shape=pltpu.VMEM((128, 1024), F32), in_s...  81.2 us

profile of v8, /device:TPU:1, one launch (start us, length us, event | category | flops | bytes accessed | tf_op | source)
XLA Modules:
  0.0 82.0 jit_solution(4081552348827195379)
XLA Ops:
  0.0 81.2 %shard_map.181 = f32[128,1024]{1,0:T(8,128)S(1)} custom-call(bf16[2,128,1024]{2,1,0:T(8,128)(2,1)} %refs_0_.1, bf16[4,128,1024]{2,1,0:T(8,128)(2,1)} %refs_1_.1, s32[2,8,128]{2,1,0:T(8,128)} %bitcast.4, s32[2,8,128]{2,1,0:T(8,128)} %bitcast.5, s32[2,8,128]{2,1,0:T(8,128)} %bitcast.6, f32[2,8,128]{2,1,0:T(8,128)} %bitcast.7, ...), custom_call_target="tpu_custom_call" | custom-call | tf_op jit(solution)/shard_map/pallas_call | solution.py:660
  81.2 0.8 copy.21
